TPU v7x, 128 devices: a whole 4x4x4 slice. The times are simulated.
128 devices in a mesh: seq: 32 (over x, z, core), tp: 4 (over y).
Axes of the slice: x: 4, y: 4, z: 4, core: 2. Of those that a mesh axis runs over, the one named last changes fastest.
Arguments:
- residual: bfloat16 [1024, 2560], P('seq', 'tp'), may hold values from -6 to 6
- queries: bfloat16 [1024, 3072], P('seq', 'tp'), may hold values from -80 to 80
- new_kv: bfloat16 [1024, 512], P('seq'), may hold values from -8 to 8
- cache: bfloat16 [2048, 256, 512], P('seq'), may hold values from -8 to 8
- out_weight: bfloat16 [3072, 2560], P('tp'), may hold values from -0.109375 to 0.109375
- block_counts: int32 [1024], replicated, may hold values from 1 to 8, 2048 in all
- last_fill: int32 [1024], replicated, may hold values from 1 to 256
- block_order: int32 [2048], P('seq'), may hold values from 0 to 2047, each once
Outputs:
- layer_out: bfloat16 [1024, 2560], P('seq', 'tp')
Inputs may be any that keep to these rules, and one draw needn't show every extreme that they name: block_counts sums to 2048, and some request has 8 blocks. last_fill of a request is the live tokens of its last block; all its other blocks are full. block_order is a permutation of the pool entries.
All inputs are finite; a program needn't handle non-finite values.
Results may differ from a plain program's by a relative error of at most 0.012.
Values may be sent and summed in bfloat16 or wider, within the bound.
A program may use at most 256 MiB of HBM per device.

v0:
```python
import jax
import jax.numpy as jnp
from jax import lax
from jax.sharding import PartitionSpec as P

very_low = -1e30


def place_blocks(block_counts, block_order):
    num_req = block_counts.shape[0]
    ends = jnp.cumsum(block_counts)
    pool_start = ends - block_counts
    block_req = jnp.sum((pool_start[None, :] <= block_order[:, None]).astype(jnp.int32), axis=1) - 1
    onehot = block_req[:, None] == jnp.arange(num_req, dtype=jnp.int32)[None, :]
    start_here = jnp.sum(jnp.where(onehot, pool_start[None, :], 0), axis=1)
    count_here = jnp.sum(jnp.where(onehot, block_counts[None, :], 0), axis=1)
    return (block_req, block_order - start_here, count_here, onehot)


def request_table(block_max, block_sum, block_acc, block_req, onehot):
    num_blocks, heads_here, head_dim = block_acc.shape
    num_req = onehot.shape[1]
    same_req = block_req[:, None] == block_req[None, :]
    max_at_block = jnp.max(jnp.where(same_req[:, :, None], block_max[None, :, :], very_low), axis=1)
    factor = jnp.exp(block_max - max_at_block)
    member = onehot.T
    cache_max = jnp.max(jnp.where(member[:, :, None], block_max[None, :, :], very_low), axis=1)
    member_float = member.astype(jnp.float32)
    cache_sum = jnp.dot(member_float, block_sum * factor, precision=lax.Precision.HIGHEST)
    scaled_acc = (block_acc * factor[:, :, None]).reshape(num_blocks, heads_here * head_dim)
    cache_acc = jnp.dot(member_float, scaled_acc, precision=lax.Precision.HIGHEST).reshape(
        num_req, heads_here, head_dim
    )
    return (cache_max, cache_sum, cache_acc)


def local(residual, queries, new_kv, cache, out_weight, block_counts, last_fill, block_order):
    rows_here = residual.shape[0]
    width_here = residual.shape[1]
    head_dim = new_kv.shape[1] // 2
    heads_here = queries.shape[1] // head_dim
    block_len = cache.shape[1]
    num_blocks = cache.shape[0]
    inv_root = 1.0 / head_dim**0.5
    query_all = lax.all_gather(queries, "seq", axis=0, tiled=True)
    block_req, block_slot, count_here, onehot = place_blocks(block_counts, block_order)
    fill_here = jnp.sum(jnp.where(onehot, last_fill[None, :], 0), axis=1)
    live_mask = (block_slot < count_here - 1)[:, None] | (
        jnp.arange(block_len, dtype=jnp.int32)[None, :] < fill_here[:, None]
    )
    query_blocks = query_all[block_req].reshape(num_blocks, heads_here, head_dim)
    keys = cache[:, :, :head_dim]
    values = cache[:, :, head_dim:]
    scores = (
        jnp.einsum("bhd,btd->bht", query_blocks, keys, preferred_element_type=jnp.float32)
        * inv_root
    )
    scores = jnp.where(live_mask[:, None, :], scores, very_low)
    block_max = jnp.max(scores, axis=2)
    weights = jnp.where(live_mask[:, None, :], jnp.exp(scores - block_max[:, :, None]), 0.0)
    block_sum = jnp.sum(weights, axis=2)
    rounded = weights.astype(jnp.bfloat16)
    block_acc = jnp.einsum("bht,btd->bhd", rounded, values, preferred_element_type=jnp.float32)
    cache_max, cache_sum, cache_acc = request_table(
        block_max, block_sum, block_acc, block_req, onehot
    )
    got_max, got_sum, got_acc = (
        lax.all_to_all(cache_max, "seq", split_axis=0, concat_axis=0, tiled=True),
        lax.all_to_all(cache_sum, "seq", split_axis=0, concat_axis=0, tiled=True),
        lax.all_to_all(cache_acc, "seq", split_axis=0, concat_axis=0, tiled=True),
    )
    sources = got_max.shape[0] // rows_here
    got_max = got_max.reshape(sources, rows_here, heads_here)
    got_sum = got_sum.reshape(sources, rows_here, heads_here)
    got_acc = got_acc.reshape(sources, rows_here, heads_here, head_dim)
    home_max = jnp.max(got_max, axis=0)
    source_factor = jnp.exp(got_max - home_max[None, :, :])
    home_sum = jnp.sum(got_sum * source_factor, axis=0)
    home_acc = jnp.sum(got_acc * source_factor[:, :, :, None], axis=0)
    query_home = queries.reshape(rows_here, heads_here, head_dim)
    own_score = (
        jnp.einsum(
            "rhd,rd->rh", query_home, new_kv[:, :head_dim], preferred_element_type=jnp.float32
        )
        * inv_root
    )
    top_score = jnp.maximum(home_max, own_score)
    cache_factor = jnp.exp(home_max - top_score)
    own_factor = jnp.exp(own_score - top_score)
    denominator = home_sum * cache_factor + own_factor
    new_value = new_kv[:, head_dim:].astype(jnp.float32)
    mixed_sum = home_acc * cache_factor[:, :, None] + own_factor[:, :, None] * new_value[:, None, :]
    attention = (
        (mixed_sum / denominator[:, :, None])
        .reshape(rows_here, heads_here * head_dim)
        .astype(jnp.bfloat16)
    )
    partial_out = jnp.dot(attention, out_weight, preferred_element_type=jnp.float32)
    summed = lax.psum(partial_out.astype(jnp.bfloat16), "tp").astype(jnp.float32)
    columns = lax.dynamic_slice_in_dim(summed, lax.axis_index("tp") * width_here, width_here, 1)
    return (residual.astype(jnp.float32) + columns).astype(jnp.bfloat16)


def solution(mesh):
    in_specs = (
        P("seq", "tp"),
        P("seq", "tp"),
        P("seq", None),
        P("seq", None, None),
        P("tp", None),
        P(),
        P(),
        P("seq"),
    )
    out_specs = P("seq", "tp")
    return jax.shard_map(local, mesh=mesh, in_specs=in_specs, out_specs=out_specs, check_vma=False)
```

profile of v0, /device:TPU:1, one launch (start us, length us, event | category | flops | bytes accessed | tf_op | source)
XLA Modules:
  0.0 206.2 jit_solution(12501185500906286605)
XLA Ops:
  6.5 0.0 all-gather.2.cloned.1.call-start
  6.5 0.7 all-gather.2.cloned.1.call-update
  7.3 1.0 reduce-window.9
  8.2 0.1 slice.19
  8.3 0.1 slice_reduce_fusion
  8.4 0.8 bitcast_subtract_fusion
  9.2 0.8 convert_reduce_fusion
  10.1 1.0 select_reduce_fusion.3
  11.1 0.7 add_compare_fusion
  11.7 0.1 broadcast_compare_fusion
  11.8 0.1 fusion.28
  11.9 0.1 iota_compare_fusion
  12.0 44.6 %all-gather.2.cloned.1.call-done = bf16[1024,768]{1,0:T(8,128)(2,1)} async-done(((bf16[32,768]{1,0:T(8,128)(2,1)}), bf16[1024,768]{1,0:T(8,128)(2,1)}) %all-gather.2.cloned.1.call-update) | async-done | bytes 1572880 | tf_op jit(solution)/shard_map/all_gather | solution.py:45
  56.7 2.4 %gather_fusion = bf16[64,768]{1,0:T(8,128)(2,1)S(1)} fusion(bf16[1024,768]{1,0:T(8,128)(2,1)} %all-gather.2.cloned.1.call-done, s32[1024]{0:T(1024)S(1)} %pad_clamp_fusion), kind=kCustom, calls=%fused_computation | custom fusion | bytes 196864 | tf_op jit(solution)/shard_map/gather | solution.py:51
  59.1 5.7 %fusion.42 = (f32[64,3]{1,0:T(8,128)S(1)}, f32[64,3,256]{2,1,0:T(4,128)S(1)}) fusion(bf16[64,3,256]{2,1,0:T(4,128)(2,1)S(1)} %reshape.170, bf16[64,256,512]{2,1,0:T(8,128)(2,1)} %param.11, pred[64,256]{1,0:T(8,128)(4,1)S(1)} %fusion.28), kind=kOutput, calls=%fused_computation.62 | convolution fusion | flops 25313088 | bytes 8700672 | tf_op jit(solution)/shard_map/bhd,btd->bht/dot_general | solution.py:55
  64.8 0.1 copy.54
  64.9 0.3 fusion.20
  65.2 0.1 select_reduce_fusion.4
  65.3 0.1 copy.55
  65.4 4.6 %fusion.8 = f32[64,3,256]{2,1,0:T(4,128)S(1)} fusion(bf16[64,256,512]{2,1,0:T(8,128)(2,1)} %param.11, f32[64,3,256]{2,1,0:T(4,128)S(1)} %get-tuple-element.16, f32[64,3]{1,0:T(8,128)S(1)} %subtract_exponential_fusion, f32[64,3]{1,0:T(8,128)S(1)} %get-tuple-element.15, pred[64,256]{1,0:T(8,128)(4,1)S(1)} %fusion.28), kind=kOutput, calls=%fused_computation.9 | convolution fusion | flops 25362432 | bytes 8799744 | tf_op jit(solution)/shard_map/bht,btd->bhd/dot_general | solution.py:63
  70.0 0.3 fusion.14
  70.3 0.1 all_to_all.18
  70.4 0.7 copy.63
  71.1 5.2 %all-to-all-start.2 = ((f32[32,32,3]{1,2,0:T(4,128)}), f32[32,32,3]{1,2,0:T(4,128)S(1)}, u32[]{:S(2)}, u32[]{:S(2)}) async-start(f32[32,32,3]{1,2,0:T(4,128)} %copy.63), calls=%async_computation.2 | async-start | bytes 131072 | tf_op jit(solution)/shard_map/all_to_all | solution.py:69
  76.3 0.2 select_reduce_fusion
  76.4 0.1 all_to_all.16
  76.5 0.7 copy.59
  77.2 6.4 %all-to-all-done.2 = f32[32,32,3]{1,2,0:T(4,128)S(1)} async-done(((f32[32,32,3]{1,2,0:T(4,128)}), f32[32,32,3]{1,2,0:T(4,128)S(1)}, u32[]{:S(2)}, u32[]{:S(2)}) %all-to-all-start.2) | async-done | bytes 12320 | tf_op jit(solution)/shard_map/all_to_all | solution.py:69
  83.6 3.9 %all-to-all-start.1 = ((f32[32,32,3]{1,2,0:T(4,128)}), f32[32,32,3]{1,2,0:T(4,128)S(1)}, u32[]{:S(2)}, u32[]{:S(2)}) async-start(f32[32,32,3]{1,2,0:T(4,128)} %copy.59), calls=%async_computation.1 | async-start | bytes 131072 | tf_op jit(solution)/shard_map/all_to_all | solution.py:68
  87.5 1.5 fusion.16
  89.1 4.1 %copy.57 = f32[1024,3,256]{2,1,0:T(4,128)} copy(f32[1024,3,256]{2,0,1:T(8,128)S(1)} %fusion.16) | data formatting | bytes 6291456 | tf_op jit(solution)/shard_map/dot_general | solution.py:31
  93.1 1.9 all-to-all-done.1
  95.0 5.8 %all-to-all-start = ((f32[1024,3,256]{2,1,0:T(4,128)}), f32[1024,3,256]{2,1,0:T(4,128)}, u32[]{:S(2)}, u32[]{:S(2)}) async-start(f32[1024,3,256]{2,1,0:T(4,128)} %copy.57), calls=%async_computation | async-start | bytes 8388608 | tf_op jit(solution)/shard_map/all_to_all | solution.py:70
  100.8 0.0 all-reduce.2.cloned.1.call-start
  100.9 0.0 copy-done.1
  100.9 0.0 copy-done.3
  100.9 0.1 fusion.33
  101.1 0.1 copy.67
  101.2 0.1 reduce_max.39
  101.3 51.8 %all-to-all-done = f32[1024,3,256]{2,1,0:T(4,128)} async-done(((f32[1024,3,256]{2,1,0:T(4,128)}), f32[1024,3,256]{2,1,0:T(4,128)}, u32[]{:S(2)}, u32[]{:S(2)}) %all-to-all-start) | async-done | bytes 3145760 | tf_op jit(solution)/shard_map/all_to_all | solution.py:70
  153.1 2.9 %fusion.4 = f32[32,3,256]{2,0,1:T(8,128)S(1)} fusion(f32[32,32,3,256]{3,2,1,0:T(4,128)} %bitcast.7, f32[32,32,3]{1,0,2:T(8,128)S(1)} %get-tuple-element.12), kind=kLoop, calls=%fused_computation.7 | loop fusion | flops 1548288 | bytes 3256320 | tf_op jit(solution)/shard_map/reduce_sum | solution.py:79
  156.0 0.1 fusion.31
  156.1 0.3 copy-done
  156.4 1.4 convolution_convert_fusion
  157.9 0.0 all-reduce.2.cloned.1.call-update
  157.9 40.1 %all-reduce.2.cloned.1.call-done = bf16[32,2560]{1,0:T(8,128)(2,1)} async-done(((bf16[32,2560]{1,0:T(8,128)(2,1)}), bf16[32,2560]{1,0:T(8,128)(2,1)}) %all-reduce.2.cloned.1.call-update) | async-done | bytes 163856 | tf_op jit(solution)/shard_map/psum | solution.py:99
  198.0 0.0 copy-done.2
  198.0 1.4 add_convert_fusion
  (15 shorter events, 0.2 us)
Async XLA Ops:
  6.5 50.1 %all-gather.2.cloned.1.call-start = ((), (), s32[]{:S(2)}) async-start(), calls=%async_computation.3 | async-start | bytes 1622016 | tf_op jit(solution)/shard_map/all_gather | solution.py:45
  71.1 12.6 %all-to-all-start.2 = ((f32[32,32,3]{1,2,0:T(4,128)}), f32[32,32,3]{1,2,0:T(4,128)S(1)}, u32[]{:S(2)}, u32[]{:S(2)}) async-start(f32[32,32,3]{1,2,0:T(4,128)} %copy.63), calls=%async_computation.2 | async-start | bytes 131072 | tf_op jit(solution)/shard_map/all_to_all | solution.py:69
  83.6 11.4 %all-to-all-start.1 = ((f32[32,32,3]{1,2,0:T(4,128)}), f32[32,32,3]{1,2,0:T(4,128)S(1)}, u32[]{:S(2)}, u32[]{:S(2)}) async-start(f32[32,32,3]{1,2,0:T(4,128)} %copy.59), calls=%async_computation.1 | async-start | bytes 131072 | tf_op jit(solution)/shard_map/all_to_all | solution.py:68
  93.1 7.7 %copy-start.1 = (bf16[32,768]{1,0:T(8,128)(2,1)S(1)}, bf16[32,768]{1,0:T(8,128)(2,1)}, u32[]{:S(2)}) copy-start(bf16[32,768]{1,0:T(8,128)(2,1)} %param.9) | copy-start | bytes 147460
  93.1 7.8 %copy-start.3 = (bf16[32,512]{1,0:T(8,128)(2,1)S(1)}, bf16[32,512]{1,0:T(8,128)(2,1)}, u32[]{:S(2)}) copy-start(bf16[32,512]{1,0:T(8,128)(2,1)} %param.10) | copy-start | bytes 98308
  95.0 58.0 %all-to-all-start = ((f32[1024,3,256]{2,1,0:T(4,128)}), f32[1024,3,256]{2,1,0:T(4,128)}, u32[]{:S(2)}, u32[]{:S(2)}) async-start(f32[1024,3,256]{2,1,0:T(4,128)} %copy.57), calls=%async_computation | async-start | bytes 8388608 | tf_op jit(solution)/shard_map/all_to_all | solution.py:70
  100.8 97.1 %all-reduce.2.cloned.1.call-start = ((), (), s32[]{:S(2)}) async-start(), calls=%async_computation.4 | async-start | bytes 327680 | tf_op jit(solution)/shard_map/psum | solution.py:99
  153.0 3.4 %copy-start = (bf16[768,2560]{1,0:T(8,128)(2,1)S(1)}, bf16[768,2560]{1,0:T(8,128)(2,1)}, u32[]{:S(2)}) copy-start(bf16[768,2560]{1,0:T(8,128)(2,1)} %param.12) | copy-start | bytes 11796484
  153.0 44.9 %copy-start.2 = (bf16[32,640]{1,0:T(8,128)(2,1)S(1)}, bf16[32,640]{1,0:T(8,128)(2,1)}, u32[]{:S(2)}) copy-start(bf16[32,640]{1,0:T(8,128)(2,1)} %param.8) | copy-start | bytes 122884
Sparse Core Ops, SparseCore 0:
  9.6 47.0 all-gather.1
  158.0 39.9 all-reduce.1
where the time goes:
time: 208 us; the launch traced here: 206 us
  waiting for transfers between devices  146 us (70%)
  starting transfers between devices  14.9 us (7%)
  matrix products  13.7 us (7%)
  between operations  13.6 us (7%)
  other arithmetic  9.63 us (5%)
  local copies, waits for them, and re-layouts  8.82 us (4%)
    all_to_all x1, waiting for transfers between devices, local(): lax.all_to_all(cache_acc, 'seq', split_axis=0, concat_axis=0, tiled=True)  51.8 us
    all_gather x1, waiting for transfers between devices, local(): query_all = lax.all_gather(queries, 'seq', axis=0, tiled=True)  44.6 us
    psum x1, waiting for transfers between devices, local(): lax.psum(partial_out.astype(jnp.bfloat16), 'tp').astype(jnp.float32)  40.1 us
    all_to_all x1, waiting for transfers between devices, local(): lax.all_to_all(cache_sum, 'seq', split_axis=0, concat_axis=0, tiled=True)  6.44 us
    all_to_all x1, starting transfers between devices, local(): lax.all_to_all(cache_acc, 'seq', split_axis=0, concat_axis=0, tiled=True)  5.81 us
    dot_general x1, matrix products, local(): jnp.einsum('bhd,btd->bht', query_blocks, keys, preferred_element_type=jnp...  5.73 us
    all_to_all x1, starting transfers between devices, local(): lax.all_to_all(cache_sum, 'seq', split_axis=0, concat_axis=0, tiled=True)  5.19 us
    dot_general x1, matrix products, local(): jnp.einsum('bht,btd->bhd', rounded, values, preferred_element_type=jnp.fl...  4.62 us
  transfers between devices with their start and end apart: 5, of which 5 were waited for; matrix products, arithmetic and copies ran while one was open for 6% of the time, Pallas kernels for 0%

commit v1 on v0

v1 whole, which is shorter than its diff:
```python
import jax
import jax.numpy as jnp
from jax import lax
from jax.experimental import pallas as pl
from jax.experimental.pallas import tpu as pltpu
from jax.sharding import PartitionSpec as P

MESH = pl.DeviceIdType.MESH
VERY_LOW = -1e30
RING = 4
GROUPS = 4


def kernel(
    order_hbm, counts_hbm, fill_hbm, residual_hbm, queries_hbm, new_kv_hbm, cache_hbm, weight_hbm,
    out_ref,
    cache, weight, residual, new_kv, q_own, counts, fill, order_all, q_all, ends_ref, starts_ref,
    onehot_ref, q_blk, live, o_scr, o_all, lse_all, tab, tab_lse, fwd, fwd_lse, home, home_lse,
    part, part_in, send_sem, recv_sem, cache_sem, local_sem,
):
    num_blocks, block_len, width = cache.shape
    head_dim = width // 2
    rows = q_own.shape[0]
    heads = q_own.shape[1] // head_dim
    cols = residual.shape[1]
    per_group = num_blocks // GROUPS
    inv_root = 1.0 / head_dim**0.5
    f32, bf16 = jnp.float32, jnp.bfloat16

    me = lax.axis_index("seq")
    tp = lax.axis_index("tp")
    core = lax.rem(me, 2)
    other = 1 - core
    chip = lax.div(me, 2)
    x = lax.div(chip, RING)
    z = lax.rem(chip, RING)
    f = x * other + z * core
    s = z * other + x * core

    def seq_of(fi, si, ci):
        xi = fi * other + si * core
        zi = si * other + fi * core
        return (xi * RING + zi) * 2 + ci

    def ring(a, k):
        return lax.rem(a + k + RING, RING)

    f_up = (seq_of(ring(f, 1), s, core), tp)
    f_dn = (seq_of(ring(f, -1), s, core), tp)
    s_up = (seq_of(f, ring(s, 1), core), tp)
    s_dn = (seq_of(f, ring(s, -1), core), tp)
    s_up_x = (seq_of(f, ring(s, 1), other), tp)
    s_dn_x = (seq_of(f, ring(s, -1), other), tp)
    f_up_x = (seq_of(ring(f, 1), s, other), tp)
    f_dn_x = (seq_of(ring(f, -1), s, other), tp)
    sib = (seq_of(f, s, other), tp)
    tps = [(me, lax.rem(tp + k, RING)) for k in range(1, RING)]

    per_copy = num_blocks // 8
    own_q = pltpu.make_async_copy(queries_hbm, q_own, local_sem.at[0])
    own_q.start()
    small = [
        pltpu.make_async_copy(order_hbm, order_all.at[f], local_sem.at[1]),
        pltpu.make_async_copy(counts_hbm, counts, local_sem.at[2]),
        pltpu.make_async_copy(fill_hbm, fill, local_sem.at[3]),
        pltpu.make_async_copy(new_kv_hbm, new_kv, local_sem.at[4]),
        pltpu.make_async_copy(residual_hbm, residual, local_sem.at[5]),
        pltpu.make_async_copy(queries_hbm, q_all.at[me], local_sem.at[6]),
    ]
    for copy in small:
        copy.start()

    barrier = pltpu.get_barrier_semaphore()
    peers = [f_up, f_dn, s_up, s_dn, s_up_x, s_dn_x, f_up_x, f_dn_x, sib] + tps
    for peer in peers:
        pl.semaphore_signal(barrier, inc=1, device_id=peer, device_id_type=MESH)

    cache_copies = [
        pltpu.make_async_copy(
            cache_hbm.at[pl.ds(i * per_copy, per_copy)],
            cache.at[pl.ds(i * per_copy, per_copy)],
            cache_sem.at[i],
        )
        for i in range(8)
    ]
    for copy in cache_copies:
        copy.start()
    weight_copies = [
        pltpu.make_async_copy(
            weight_hbm.at[:, pl.ds(t * cols, cols)], weight.at[t], local_sem.at[7 + t]
        )
        for t in range(RING)
    ]
    for copy in weight_copies:
        copy.start()

    started = []

    def send(src, dst, peer):
        n = len(started)
        copy = pltpu.make_async_remote_copy(
            src_ref=src, dst_ref=dst, send_sem=send_sem.at[n], recv_sem=recv_sem.at[n],
            device_id=peer, device_id_type=MESH,
        )
        copy.start()
        started.append(copy)
        return copy

    own_q.wait()
    pl.semaphore_wait(barrier, len(peers))

    half = rows // 2
    top, bottom = pl.ds(0, half), pl.ds(half, half)

    def chunk(i, j):
        return q_all.at[seq_of(ring(f, i), ring(s, j), core)]

    def part_of(i, j, which):
        return q_all.at[seq_of(ring(f, i), ring(s, j), core), which]

    sib_copies = []

    def to_sib(i, j, src=None):
        c = chunk(i, j)
        sib_copies.append(send(c if src is None else src, c, sib))

    def to_s(i, src=None):
        c = chunk(i, 0)
        return (send(c if src is None else src, c, s_up), send(c if src is None else src, c, s_dn))

    own_up = send(q_own, chunk(0, 0), f_up)
    own_dn = send(q_own, chunk(0, 0), f_dn)
    s_copies = {0: to_s(0, q_own)}
    order_own = order_all.at[f]
    to_sib(0, 0, q_own)

    for copy in small:
        copy.wait()
    order_up = send(order_own, order_own, f_up)
    order_dn = send(order_own, order_own, f_dn)

    counts_f = counts[...].astype(f32)
    fill_f = fill[...].astype(f32)
    lane_n = counts_f.shape[1]
    sub_i = lax.broadcasted_iota(jnp.int32, (lane_n, lane_n), 0)
    lane_i = lax.broadcasted_iota(jnp.int32, (lane_n, lane_n), 1)
    upper = (sub_i <= lane_i).astype(f32).astype(bf16)
    cum = jnp.dot(counts_f.astype(bf16), upper, preferred_element_type=f32)
    before = jnp.zeros((1, 1), f32)
    pieces = counts_f.shape[0]
    for k in range(pieces):
        ends_k = cum[k:k + 1, :] + before
        ends_ref[k:k + 1, :] = ends_k
        starts_ref[k:k + 1, :] = ends_k - counts_f[k:k + 1, :]
        before = before + jnp.sum(counts_f[k:k + 1, :], axis=1, keepdims=True)

    sub64 = lax.broadcasted_iota(jnp.int32, (num_blocks, num_blocks), 0)
    lane64 = lax.broadcasted_iota(jnp.int32, (num_blocks, num_blocks), 1)
    order_row = order_all[f].astype(f32)
    order_col = jnp.sum(
        jnp.where(sub64 == lane64, jnp.broadcast_to(order_row, (num_blocks, num_blocks)), 0.0),
        axis=1, keepdims=True,
    )
    fill_raw = jnp.zeros((num_blocks, lane_n), f32)
    for k in range(pieces):
        ends_k = ends_ref[k:k + 1, :]
        starts_k = starts_ref[k:k + 1, :]
        hit = (starts_k <= order_col) & (order_col < ends_k)
        onehot_ref[:, k * lane_n:(k + 1) * lane_n] = jnp.where(hit, 1.0, 0.0).astype(bf16)
        fill_raw = fill_raw + jnp.where(ends_k == order_col + 1.0, fill_f[k:k + 1, :], 0.0)
    fill_sum = jnp.sum(fill_raw, axis=1, keepdims=True)
    live_n = jnp.where(fill_sum > 0.0, fill_sum, float(block_len))
    for h in range(8):
        live[:, h, :] = jnp.broadcast_to(live_n, (num_blocks, block_len))
    q_blk[...] = jnp.zeros(q_blk.shape, f32)

    own_up.wait_recv()
    fwd_up = send(part_of(-1, 0, top), part_of(-1, 0, top), f_up)
    s_copies[-1] = to_s(-1)
    own_dn.wait_recv()
    fwd_dn = send(part_of(1, 0, bottom), part_of(1, 0, bottom), f_dn)
    s_copies[1] = to_s(1)
    to_sib(-1, 0)
    to_sib(1, 0)
    order_up.wait_recv()
    order_dn.wait_recv()
    order_from = order_all.at[ring(f, -1)]
    order_fwd = send(order_from, order_from, f_up)

    s_fwd = {}

    def forward_s(i):
        up, dn = s_copies[i]
        up.wait_recv()
        a = send(part_of(i, -1, top), part_of(i, -1, top), s_up)
        dn.wait_recv()
        b = send(part_of(i, 1, bottom), part_of(i, 1, bottom), s_dn)
        s_fwd[i] = (a, b)
        to_sib(i, -1)
        to_sib(i, 1)

    forward_s(0)
    fwd_up.wait_recv()
    fwd_dn.wait_recv()
    s_copies[2] = to_s(2)
    to_sib(2, 0)
    forward_s(-1)
    forward_s(1)
    for copy in s_fwd[0]:
        copy.wait_recv()
    to_sib(0, 2)
    forward_s(2)
    for i in (-1, 1, 2):
        for copy in s_fwd[i]:
            copy.wait_recv()
        to_sib(i, 2)
    for copy in sib_copies:
        copy.wait_recv()

    picked = jnp.dot(
        onehot_ref[...], q_all[...].reshape(q_all.shape[0] * rows, heads * head_dim),
        preferred_element_type=f32,
    )
    for h in range(heads):
        q_blk[:, h, :] = picked[:, h * head_dim:(h + 1) * head_dim]

    lse_all[f] = jnp.zeros((8, lane_n), f32)
    token = lax.broadcasted_iota(jnp.int32, (8, block_len), 1).astype(f32)
    lane8 = lax.broadcasted_iota(jnp.int32, (8, lane_n), 1)
    o_sends, o_fwds = [], []

    def forward_o(g):
        up, dn = o_sends[g]
        up.wait_recv()
        dn.wait_recv()
        if g % 2 == 0:
            ref = o_all.at[ring(f, -1), g]
            o_fwds.append(send(ref, ref, f_up))
        else:
            ref = o_all.at[ring(f, 1), g]
            o_fwds.append(send(ref, ref, f_dn))

    for g in range(GROUPS):
        for i in range(8 // GROUPS):
            cache_copies[g * (8 // GROUPS) + i].wait()
        blocks = range(g * per_group, (g + 1) * per_group)
        lse_rows = lse_all[f]
        scores = []
        for b in blocks:
            q8 = q_blk[b].astype(bf16)
            scores.append(
                lax.dot_general(
                    q8, cache[b, :, :head_dim], (((1,), (1,)), ((), ())), preferred_element_type=f32
                )
            )
        for b, score in zip(blocks, scores):
            alive = token < live[b]
            score = jnp.where(alive, score * inv_root, VERY_LOW)
            top_b = jnp.max(score, axis=1, keepdims=True)
            w = jnp.where(alive, jnp.exp(score - top_b), 0.0)
            total = jnp.sum(w, axis=1, keepdims=True)
            acc = jnp.dot(w.astype(bf16), cache[b, :, head_dim:], preferred_element_type=f32)
            o_scr[b] = acc / total
            lse_rows = jnp.where(lane8 == b, top_b + jnp.log(total), lse_rows)
        lse_all[f] = lse_rows
        for h in range(heads):
            o_all[f, g, :, h * head_dim:(h + 1) * head_dim] = (
                o_scr[g * per_group:(g + 1) * per_group, h, :].astype(bf16)
            )
        ref = o_all.at[f, g]
        o_sends.append((send(ref, ref, f_up), send(ref, ref, f_dn)))
        if g >= 2:
            forward_o(g - 2)
    ref = lse_all.at[f]
    lse_up, lse_dn = send(ref, ref, f_up), send(ref, ref, f_dn)

    q_f = q_own[...].astype(f32)
    new_key = new_kv[:, :head_dim].astype(f32)
    own_score = [
        jnp.sum(q_f[:, h * head_dim:(h + 1) * head_dim] * new_key, axis=1, keepdims=True) * inv_root
        for h in range(heads)
    ]
    for copy in weight_copies:
        copy.wait()

    forward_o(GROUPS - 2)
    forward_o(GROUPS - 1)
    lse_up.wait_recv()
    lse_dn.wait_recv()
    ref = lse_all.at[ring(f, -1)]
    lse_fwd = send(ref, ref, f_up)
    order_fwd.wait_recv()
    for copy in o_fwds:
        copy.wait_recv()
    lse_fwd.wait_recv()

    def pair(a, b):
        lanes = lax.broadcasted_iota(jnp.int32, a.shape, 1)
        return jnp.where(lanes < num_blocks, a, pltpu.roll(b, num_blocks, 1))

    lse = jnp.concatenate(
        [pair(lse_all[0], lse_all[1]), pair(lse_all[2], lse_all[3])], axis=1
    )

    def order_pair(a, b):
        return jnp.concatenate([order_all[a].astype(f32), order_all[b].astype(f32)], axis=1)

    order_lanes = jnp.concatenate([order_pair(0, 1), order_pair(2, 3)], axis=1)
    o_rows = o_all[...].reshape(RING * num_blocks, heads * head_dim)
    places = 2 * rows
    sub_p = lax.broadcasted_iota(jnp.int32, (places, lane_n), 0)
    lane_p = lax.broadcasted_iota(jnp.int32, (places, lane_n), 1)
    row8 = lax.broadcasted_iota(jnp.int32, (8, lane_n), 0)

    def column(j):
        first = (RING * places * f + places * j) * other + (RING * places * j + places * f) * core
        piece = lax.div(first, lane_n)
        offset = lax.rem(first, lane_n)
        diag = lane_p == sub_p + offset
        end = jnp.sum(jnp.where(diag, ends_ref[pl.ds(piece, 1), :], 0.0), axis=1, keepdims=True)
        start = jnp.sum(jnp.where(diag, starts_ref[pl.ds(piece, 1), :], 0.0), axis=1, keepdims=True)
        member = (start <= order_lanes) & (order_lanes < end)
        tile = jnp.zeros((8, lane_n), f32)
        for h in range(heads):
            here = jnp.where(member, lse[h:h + 1, :], VERY_LOW)
            top_r = jnp.max(here, axis=1, keepdims=True)
            w = jnp.where(member, jnp.exp(here - top_r), 0.0).astype(bf16)
            total = jnp.sum(w.astype(f32), axis=1, keepdims=True)
            acc = jnp.dot(
                w, o_rows[:, h * head_dim:(h + 1) * head_dim], preferred_element_type=f32
            )
            safe = jnp.where(total > 0.0, total, 1.0)
            tab[j, :, h * head_dim:(h + 1) * head_dim] = (acc / safe).astype(bf16)
            lse_r = jnp.where(total > 0.0, top_r + jnp.log(safe), VERY_LOW)
            row = jnp.sum(jnp.where(lane_p == sub_p, lse_r, 0.0), axis=0, keepdims=True)
            tile = jnp.where(row8 == h, row, tile)
        tab_lse[j] = tile

    def rows_of(j, c):
        return tab.at[j, pl.ds(pl.multiple_of(c * rows, rows), rows)]

    slot = core * RING + s
    arrivals = []
    j = ring(s, 2)
    column(j)
    via = [
        send(rows_of(j, core), fwd.at[0], s_up), send(tab_lse.at[j], fwd_lse.at[0], s_up),
        send(rows_of(j, other), fwd.at[1], s_dn), send(tab_lse.at[j], fwd_lse.at[1], s_dn),
    ]
    for k, same, cross in ((1, s_up, s_up_x), (-1, s_dn, s_dn_x)):
        j = ring(s, k)
        column(j)
        arrivals += [
            send(rows_of(j, core), home.at[slot], same),
            send(tab_lse.at[j], home_lse.at[slot], same),
            send(rows_of(j, other), home.at[slot], cross),
            send(tab_lse.at[j], home_lse.at[slot], cross),
        ]
    column(s)
    arrivals += [
        send(rows_of(s, other), home.at[slot], sib), send(tab_lse.at[s], home_lse.at[slot], sib)
    ]
    for copy in via:
        copy.wait_recv()
    up_slot = core * RING + ring(s, -1)
    dn_slot = core * RING + ring(s, 1)
    arrivals += [
        send(fwd.at[0], home.at[up_slot], s_up), send(fwd_lse.at[0], home_lse.at[up_slot], s_up),
        send(fwd.at[1], home.at[dn_slot], s_dn_x), send(fwd_lse.at[1], home_lse.at[dn_slot], s_dn_x),
    ]
    home[slot] = tab[s, pl.ds(pl.multiple_of(core * rows, rows), rows)]
    home_lse[slot] = tab_lse[s]
    for copy in arrivals:
        copy.wait_recv()

    sub_r = lax.broadcasted_iota(jnp.int32, (rows, lane_n), 0)
    lane_r = lax.broadcasted_iota(jnp.int32, (rows, lane_n), 1)
    diag = lane_r == sub_r + core * rows
    new_value = new_kv[:, head_dim:].astype(f32)
    attention = []
    sources = 2 * RING
    for h in range(heads):
        cols_h = [
            jnp.sum(jnp.where(diag, home_lse[n, h:h + 1, :], 0.0), axis=1, keepdims=True)
            for n in range(sources)
        ]
        top_h = own_score[h]
        for c in cols_h:
            top_h = jnp.maximum(top_h, c)
        w = jnp.exp(own_score[h] - top_h)
        mixed, denominator = w * new_value, w
        for n in range(sources):
            w = jnp.exp(cols_h[n] - top_h)
            denominator = denominator + w
            mixed = mixed + w * home[n, :, h * head_dim:(h + 1) * head_dim].astype(f32)
        attention.append((mixed / denominator).astype(bf16))
    att = jnp.concatenate(attention, axis=1)

    tp_sends = []
    for k in (2, 1, 3):
        t = lax.rem(tp + k, RING)
        part[t] = jnp.dot(att, weight[t], preferred_element_type=f32).astype(bf16)
        tp_sends.append(send(part.at[t], part_in.at[tp], tps[k - 1]))
    total = jnp.dot(att, weight[tp], preferred_element_type=f32) + residual[...].astype(f32)
    for copy in tp_sends:
        copy.wait_recv()
    for k in range(1, RING):
        total = total + part_in[lax.rem(tp + k, RING)].astype(f32)
    out_ref[...] = total.astype(bf16)

    for copy in started:
        copy.wait_send()


def local(residual, queries, new_kv, cache, out_weight, block_counts, last_fill, block_order):
    rows, cols = residual.shape
    num_blocks, block_len, width = cache.shape
    head_dim = width // 2
    q_cols = queries.shape[1]
    requests = block_counts.shape[0]
    lanes = 128
    devices = requests // rows
    any_spec = pl.BlockSpec(memory_space=pl.ANY)
    f32, bf16 = jnp.float32, jnp.bfloat16
    copies = 96
    return pl.pallas_call(
        kernel,
        out_shape=jax.ShapeDtypeStruct((rows, cols), bf16),
        in_specs=[any_spec] * 8,
        out_specs=pl.BlockSpec(memory_space=pltpu.VMEM),
        scratch_shapes=[
            pltpu.VMEM(cache.shape, bf16),
            pltpu.VMEM((RING, q_cols, cols), bf16),
            pltpu.VMEM((rows, cols), bf16),
            pltpu.VMEM((rows, width), bf16),
            pltpu.VMEM((rows, q_cols), bf16),
            pltpu.VMEM((requests // lanes, lanes), jnp.int32),
            pltpu.VMEM((requests // lanes, lanes), jnp.int32),
            pltpu.VMEM((RING, 1, num_blocks), jnp.int32),
            pltpu.VMEM((devices, rows, q_cols), bf16),
            pltpu.VMEM((requests // lanes, lanes), f32),
            pltpu.VMEM((requests // lanes, lanes), f32),
            pltpu.VMEM((num_blocks, requests), bf16),
            pltpu.VMEM((num_blocks, 8, head_dim), f32),
            pltpu.VMEM((num_blocks, 8, block_len), f32),
            pltpu.VMEM((num_blocks, 8, head_dim), f32),
            pltpu.VMEM((RING, GROUPS, num_blocks // GROUPS, q_cols), bf16),
            pltpu.VMEM((RING, 8, lanes), f32),
            pltpu.VMEM((RING, 2 * rows, q_cols), bf16),
            pltpu.VMEM((RING, 8, lanes), f32),
            pltpu.VMEM((2, rows, q_cols), bf16),
            pltpu.VMEM((2, 8, lanes), f32),
            pltpu.VMEM((2 * RING, rows, q_cols), bf16),
            pltpu.VMEM((2 * RING, 8, lanes), f32),
            pltpu.VMEM((RING, rows, cols), bf16),
            pltpu.VMEM((RING, rows, cols), bf16),
            pltpu.SemaphoreType.DMA((copies,)),
            pltpu.SemaphoreType.DMA((copies,)),
            pltpu.SemaphoreType.DMA((8,)),
            pltpu.SemaphoreType.DMA((11,)),
        ],
        compiler_params=pltpu.CompilerParams(
            collective_id=0, has_side_effects=True, vmem_limit_bytes=60 * 1024 * 1024
        ),
    )(
        block_order.reshape(1, num_blocks),
        block_counts.reshape(requests // lanes, lanes),
        last_fill.reshape(requests // lanes, lanes),
        residual, queries, new_kv, cache, out_weight,
    )


def solution(mesh):
    in_specs = (
        P("seq", "tp"), P("seq", "tp"), P("seq", None), P("seq", None, None), P("tp", None),
        P(), P(), P("seq"),
    )
    return jax.shard_map(
        local, mesh=mesh, in_specs=in_specs, out_specs=P("seq", "tp"), check_vma=False
    )
```

time: 208 us -> 49.2 us (0.24)
  waiting for transfers between devices: 146 us -> 0 us
  Pallas kernels: 0 us -> 47.1 us
  starting transfers between devices: 14.9 us -> 0 us
  matrix products: 13.7 us -> 0 us
  between operations: 13.6 us -> 0.01 us
  other arithmetic: 9.63 us -> 0 us
  local copies, waits for them, and re-layouts: 8.82 us -> 1.4 us
    all_to_all x3 -> x0, waiting for transfers between devices: 60.1 us -> none  [the longest x1 51.8 us: local(): lax.all_to_all(cache_acc, 'seq', split_axis=0, concat_axis=0, tiled=True)]
    pallas_call x0 -> x1, Pallas kernels: none -> 47.1 us  [local(): pl.pallas_call(kernel, out_shape=jax.ShapeDtypeStruct((rows, cols), bf16)...]
    all_gather x1 -> x0, waiting for transfers between devices: 44.6 us -> none  [local(): query_all = lax.all_gather(queries, 'seq', axis=0, tiled=True)]
    psum x1 -> x0, waiting for transfers between devices: 40.1 us -> none  [local(): lax.psum(partial_out.astype(jnp.bfloat16), 'tp').astype(jnp.float32)]
    all_to_all x3 -> x0, starting transfers between devices: 14.9 us -> none  [the longest x1 5.81 us: local(): lax.all_to_all(cache_acc, 'seq', split_axis=0, concat_axis=0, tiled=True)]
    dot_general x6 -> x0, matrix products: 13.7 us -> none  [the longest x1 5.73 us: local(): jnp.einsum('bhd,btd->bht', query_blocks, keys, preferred_element_type=jnp...]
    reduce_sum x5 -> x0, other arithmetic: 5.05 us -> none  [the longest x1 2.9 us: local(): home_acc = jnp.sum(got_acc * source_factor[:, :, :, None], axis=0)]
    dot_general x2 -> x0, local copies, waits for them, and re-layouts: 4.16 us -> none  [the longest x1 4.08 us: request_table(): jnp.dot(member_float, scaled_acc, precision=lax.Precision.HIGHEST)]
  transfers between devices with their start and end apart: 5 -> 0, of which waited for: 5 -> 0; matrix products, arithmetic and copies ran while one was open for 6% -> 0% of each run, Pallas kernels for 0% -> 0%
where the time goes in v1:
time: 49.2 us; the launch traced here: 48.5 us
  Pallas kernels  47.1 us (96%)
  local copies, waits for them, and re-layouts  1.4 us (3%)
    pallas_call x1, Pallas kernels, local(): pl.pallas_call(kernel, out_shape=jax.ShapeDtypeStruct((rows, cols), bf16)...  47.1 us
    unnamed x1, local copies, waits for them, and re-layouts  1.4 us

profile of v1, /device:TPU:1, one launch (start us, length us, event | category | flops | bytes accessed | tf_op | source)
XLA Modules:
  0.0 48.5 jit_solution(16723484050633930096)
XLA Ops:
  0.0 47.1 %shard_map.82 = bf16[32,640]{1,0:T(8,128)(2,1)} custom-call(s32[1,64]{1,0:T(1,128)} %bitcast.5, s32[8,128]{1,0:T(8,128)} %bitcast.3, s32[8,128]{1,0:T(8,128)} %bitcast.4, bf16[32,640]{1,0:T(8,128)(2,1)} %residual_hbm.1, bf16[32,768]{1,0:T(8,128)(2,1)} %queries_hbm.1, bf16[32,512]{1,0:T(8,128)(2,1)} %new_kv_hbm.1, bf16[64,256,512]{2,1,0:T(8,128)(2,1)} %cache_hbm.1, ...), custom_call_target="tpu_custom_call" | custom-call | tf_op jit(solution)/shard_map/pallas_call | solution.py:426
  47.1 1.4 %copy.10 = bf16[32,640]{1,0:T(8,128)(2,1)} copy(bf16[32,640]{1,0:T(8,128)(2,1)} %shard_map.82) | data formatting | bytes 81920

commit v2 on v1

--- a/solution.py
+++ b/solution.py
@@ -15,8 +15,8 @@
     order_hbm, counts_hbm, fill_hbm, residual_hbm, queries_hbm, new_kv_hbm, cache_hbm, weight_hbm,
     out_ref,
     cache, weight, residual, new_kv, q_own, counts, fill, order_all, q_all, ends_ref, starts_ref,
-    onehot_ref, q_blk, live, o_scr, o_all, lse_all, tab, tab_lse, fwd, fwd_lse, home, home_lse,
-    part, part_in, send_sem, recv_sem, cache_sem, local_sem,
+    onehot_ref, order_sib, pick_out, pick_in, q_blk, live, o_scr, o_all, lse_all, tab, tab_lse,
+    home, home_lse, part, part_in, send_sem, recv_sem, cache_sem, local_sem,
 ):
     num_blocks, block_len, width = cache.shape
     head_dim = width // 2
@@ -51,12 +51,22 @@
     s_dn = (seq_of(f, ring(s, -1), core), tp)
     s_up_x = (seq_of(f, ring(s, 1), other), tp)
     s_dn_x = (seq_of(f, ring(s, -1), other), tp)
+    f_2 = (seq_of(ring(f, 2), s, core), tp)
+    s_2 = (seq_of(f, ring(s, 2), core), tp)
+    s_2_x = (seq_of(f, ring(s, 2), other), tp)
     f_up_x = (seq_of(ring(f, 1), s, other), tp)
     f_dn_x = (seq_of(ring(f, -1), s, other), tp)
+    f_2_x = (seq_of(ring(f, 2), s, other), tp)
     sib = (seq_of(f, s, other), tp)
     tps = [(me, lax.rem(tp + k, RING)) for k in range(1, RING)]
 
-    per_copy = num_blocks // 8
+    barrier = pltpu.get_barrier_semaphore()
+    peers = [
+        f_up, f_dn, f_2, s_up, s_dn, s_2, f_up_x, f_dn_x, f_2_x, s_up_x, s_dn_x, s_2_x, sib
+    ] + tps
+    for peer in peers:
+        pl.semaphore_signal(barrier, inc=1, device_id=peer, device_id_type=MESH)
+
     own_q = pltpu.make_async_copy(queries_hbm, q_own, local_sem.at[0])
     own_q.start()
     small = [
@@ -70,41 +80,35 @@
     for copy in small:
         copy.start()
 
-    barrier = pltpu.get_barrier_semaphore()
-    peers = [f_up, f_dn, s_up, s_dn, s_up_x, s_dn_x, f_up_x, f_dn_x, sib] + tps
-    for peer in peers:
-        pl.semaphore_signal(barrier, inc=1, device_id=peer, device_id_type=MESH)
-
     cache_copies = [
         pltpu.make_async_copy(
-            cache_hbm.at[pl.ds(i * per_copy, per_copy)],
-            cache.at[pl.ds(i * per_copy, per_copy)],
+            cache_hbm.at[pl.ds(i * per_group, per_group)],
+            cache.at[pl.ds(i * per_group, per_group)],
             cache_sem.at[i],
         )
-        for i in range(8)
+        for i in range(GROUPS)
     ]
     for copy in cache_copies:
         copy.start()
     weight_copies = [
         pltpu.make_async_copy(
-            weight_hbm.at[:, pl.ds(t * cols, cols)], weight.at[t], local_sem.at[7 + t]
+            weight_hbm.at[:, pl.ds(t * cols, cols)], weight.at[t], local_sem.at[7]
         )
         for t in range(RING)
     ]
     for copy in weight_copies:
         copy.start()
 
-    started = []
-
-    def send(src, dst, peer):
-        n = len(started)
+    def send(src, dst, peer, ss, rs):
         copy = pltpu.make_async_remote_copy(
-            src_ref=src, dst_ref=dst, send_sem=send_sem.at[n], recv_sem=recv_sem.at[n],
+            src_ref=src, dst_ref=dst, send_sem=send_sem.at[ss], recv_sem=recv_sem.at[rs],
             device_id=peer, device_id_type=MESH,
         )
         copy.start()
-        started.append(copy)
         return copy
+
+    def wait_bytes(ref, sem):
+        pltpu.make_async_copy(ref, ref, sem).wait()
 
     own_q.wait()
     pl.semaphore_wait(barrier, len(peers))
@@ -118,26 +122,24 @@
     def part_of(i, j, which):
         return q_all.at[seq_of(ring(f, i), ring(s, j), core), which]
 
-    sib_copies = []
-
-    def to_sib(i, j, src=None):
-        c = chunk(i, j)
-        sib_copies.append(send(c if src is None else src, c, sib))
-
     def to_s(i, src=None):
         c = chunk(i, 0)
-        return (send(c if src is None else src, c, s_up), send(c if src is None else src, c, s_dn))
-
-    own_up = send(q_own, chunk(0, 0), f_up)
-    own_dn = send(q_own, chunk(0, 0), f_dn)
+        src = c if src is None else src
+        n = 3 + 2 * (i % RING)
+        return (send(src, c, s_up, 0, n), send(src, c, s_dn, 0, n + 1))
+
+    own_up = send(q_own, chunk(0, 0), f_up, 0, 0)
+    own_dn = send(q_own, chunk(0, 0), f_dn, 0, 1)
+    own_2 = send(q_own, chunk(0, 0), f_2, 0, 2)
     s_copies = {0: to_s(0, q_own)}
-    order_own = order_all.at[f]
-    to_sib(0, 0, q_own)
 
     for copy in small:
         copy.wait()
-    order_up = send(order_own, order_own, f_up)
-    order_dn = send(order_own, order_own, f_dn)
+    order_own = order_all.at[f]
+    order_to_sib = send(order_own, order_sib, sib, 1, 12)
+    order_copies = [
+        send(order_own, order_own, peer, 2 + k, 13 + k) for k, peer in enumerate((f_up, f_dn, f_2))
+    ]
 
     counts_f = counts[...].astype(f32)
     fill_f = fill[...].astype(f32)
@@ -156,93 +158,70 @@
 
     sub64 = lax.broadcasted_iota(jnp.int32, (num_blocks, num_blocks), 0)
     lane64 = lax.broadcasted_iota(jnp.int32, (num_blocks, num_blocks), 1)
-    order_row = order_all[f].astype(f32)
-    order_col = jnp.sum(
-        jnp.where(sub64 == lane64, jnp.broadcast_to(order_row, (num_blocks, num_blocks)), 0.0),
-        axis=1, keepdims=True,
-    )
+
+    def column_of(order_row):
+        return jnp.sum(
+            jnp.where(
+                sub64 == lane64, jnp.broadcast_to(order_row, (num_blocks, num_blocks)), 0.0
+            ),
+            axis=1, keepdims=True,
+        )
+
+    order_col = column_of(order_all[f].astype(f32))
     fill_raw = jnp.zeros((num_blocks, lane_n), f32)
     for k in range(pieces):
         ends_k = ends_ref[k:k + 1, :]
         starts_k = starts_ref[k:k + 1, :]
         hit = (starts_k <= order_col) & (order_col < ends_k)
-        onehot_ref[:, k * lane_n:(k + 1) * lane_n] = jnp.where(hit, 1.0, 0.0).astype(bf16)
+        onehot_ref[0, :, k * lane_n:(k + 1) * lane_n] = jnp.where(hit, 1.0, 0.0).astype(bf16)
         fill_raw = fill_raw + jnp.where(ends_k == order_col + 1.0, fill_f[k:k + 1, :], 0.0)
     fill_sum = jnp.sum(fill_raw, axis=1, keepdims=True)
     live_n = jnp.where(fill_sum > 0.0, fill_sum, float(block_len))
+    order_to_sib.wait_recv()
+    order_col = column_of(order_sib[...].astype(f32))
+    for k in range(pieces):
+        hit = (starts_ref[k:k + 1, :] <= order_col) & (order_col < ends_ref[k:k + 1, :])
+        onehot_ref[1, :, k * lane_n:(k + 1) * lane_n] = jnp.where(hit, 1.0, 0.0).astype(bf16)
+    for n in range(RING * RING):
+        q_all[2 * n + other] = jnp.zeros((rows, heads * head_dim), bf16)
     for h in range(8):
         live[:, h, :] = jnp.broadcast_to(live_n, (num_blocks, block_len))
     q_blk[...] = jnp.zeros(q_blk.shape, f32)
 
-    own_up.wait_recv()
-    fwd_up = send(part_of(-1, 0, top), part_of(-1, 0, top), f_up)
-    s_copies[-1] = to_s(-1)
-    own_dn.wait_recv()
-    fwd_dn = send(part_of(1, 0, bottom), part_of(1, 0, bottom), f_dn)
-    s_copies[1] = to_s(1)
-    to_sib(-1, 0)
-    to_sib(1, 0)
-    order_up.wait_recv()
-    order_dn.wait_recv()
-    order_from = order_all.at[ring(f, -1)]
-    order_fwd = send(order_from, order_from, f_up)
-
-    s_fwd = {}
-
     def forward_s(i):
         up, dn = s_copies[i]
         up.wait_recv()
-        a = send(part_of(i, -1, top), part_of(i, -1, top), s_up)
+        send(part_of(i, -1, top), part_of(i, -1, top), s_up, 0, 11)
         dn.wait_recv()
-        b = send(part_of(i, 1, bottom), part_of(i, 1, bottom), s_dn)
-        s_fwd[i] = (a, b)
-        to_sib(i, -1)
-        to_sib(i, 1)
-
+        send(part_of(i, 1, bottom), part_of(i, 1, bottom), s_dn, 0, 11)
+
+    own_up.wait_recv()
+    s_copies[-1] = to_s(-1)
+    own_dn.wait_recv()
+    s_copies[1] = to_s(1)
     forward_s(0)
-    fwd_up.wait_recv()
-    fwd_dn.wait_recv()
+    own_2.wait_recv()
     s_copies[2] = to_s(2)
-    to_sib(2, 0)
     forward_s(-1)
     forward_s(1)
-    for copy in s_fwd[0]:
-        copy.wait_recv()
-    to_sib(0, 2)
     forward_s(2)
-    for i in (-1, 1, 2):
-        for copy in s_fwd[i]:
-            copy.wait_recv()
-        to_sib(i, 2)
-    for copy in sib_copies:
-        copy.wait_recv()
-
-    picked = jnp.dot(
-        onehot_ref[...], q_all[...].reshape(q_all.shape[0] * rows, heads * head_dim),
-        preferred_element_type=f32,
-    )
+    wait_bytes(q_all.at[pl.ds(0, RING)], recv_sem.at[11])
+
+    q_rows = q_all[...].reshape(q_all.shape[0] * rows, heads * head_dim)
+    pick_out[...] = jnp.dot(onehot_ref[1], q_rows, preferred_element_type=f32).astype(bf16)
+    pick = send(pick_out, pick_in, sib, 5, 16)
+    picked = jnp.dot(onehot_ref[0], q_rows, preferred_element_type=f32)
+    pick.wait_recv()
+    picked = picked + pick_in[...].astype(f32)
     for h in range(heads):
         q_blk[:, h, :] = picked[:, h * head_dim:(h + 1) * head_dim]
 
     lse_all[f] = jnp.zeros((8, lane_n), f32)
     token = lax.broadcasted_iota(jnp.int32, (8, block_len), 1).astype(f32)
     lane8 = lax.broadcasted_iota(jnp.int32, (8, lane_n), 1)
-    o_sends, o_fwds = [], []
-
-    def forward_o(g):
-        up, dn = o_sends[g]
-        up.wait_recv()
-        dn.wait_recv()
-        if g % 2 == 0:
-            ref = o_all.at[ring(f, -1), g]
-            o_fwds.append(send(ref, ref, f_up))
-        else:
-            ref = o_all.at[ring(f, 1), g]
-            o_fwds.append(send(ref, ref, f_dn))
 
     for g in range(GROUPS):
-        for i in range(8 // GROUPS):
-            cache_copies[g * (8 // GROUPS) + i].wait()
+        cache_copies[g].wait()
         blocks = range(g * per_group, (g + 1) * per_group)
         lse_rows = lse_all[f]
         scores = []
@@ -268,11 +247,11 @@
                 o_scr[g * per_group:(g + 1) * per_group, h, :].astype(bf16)
             )
         ref = o_all.at[f, g]
-        o_sends.append((send(ref, ref, f_up), send(ref, ref, f_dn)))
-        if g >= 2:
-            forward_o(g - 2)
+        for peer in (f_2, f_up, f_dn):
+            send(ref, ref, peer, 6, 17)
     ref = lse_all.at[f]
-    lse_up, lse_dn = send(ref, ref, f_up), send(ref, ref, f_dn)
+    for peer in (f_2, f_up, f_dn):
+        send(ref, ref, peer, 7, 18)
 
     q_f = q_own[...].astype(f32)
     new_key = new_kv[:, :head_dim].astype(f32)
@@ -280,19 +259,11 @@
         jnp.sum(q_f[:, h * head_dim:(h + 1) * head_dim] * new_key, axis=1, keepdims=True) * inv_root
         for h in range(heads)
     ]
-    for copy in weight_copies:
-        copy.wait()
-
-    forward_o(GROUPS - 2)
-    forward_o(GROUPS - 1)
-    lse_up.wait_recv()
-    lse_dn.wait_recv()
-    ref = lse_all.at[ring(f, -1)]
-    lse_fwd = send(ref, ref, f_up)
-    order_fwd.wait_recv()
-    for copy in o_fwds:
+    wait_bytes(weight, local_sem.at[7])
+    for copy in order_copies:
         copy.wait_recv()
-    lse_fwd.wait_recv()
+    wait_bytes(lse_all.at[pl.ds(0, RING - 1)], recv_sem.at[18])
+    wait_bytes(o_all.at[pl.ds(0, RING - 1)], recv_sem.at[17])
 
     def pair(a, b):
         lanes = lax.broadcasted_iota(jnp.int32, a.shape, 1)
@@ -340,45 +311,27 @@
         return tab.at[j, pl.ds(pl.multiple_of(c * rows, rows), rows)]
 
     slot = core * RING + s
-    arrivals = []
-    j = ring(s, 2)
-    column(j)
-    via = [
-        send(rows_of(j, core), fwd.at[0], s_up), send(tab_lse.at[j], fwd_lse.at[0], s_up),
-        send(rows_of(j, other), fwd.at[1], s_dn), send(tab_lse.at[j], fwd_lse.at[1], s_dn),
-    ]
-    for k, same, cross in ((1, s_up, s_up_x), (-1, s_dn, s_dn_x)):
+    for k, same, cross in ((2, s_2, s_2_x), (1, s_up, s_up_x), (-1, s_dn, s_dn_x)):
         j = ring(s, k)
         column(j)
-        arrivals += [
-            send(rows_of(j, core), home.at[slot], same),
-            send(tab_lse.at[j], home_lse.at[slot], same),
-            send(rows_of(j, other), home.at[slot], cross),
-            send(tab_lse.at[j], home_lse.at[slot], cross),
-        ]
+        send(rows_of(j, core), home.at[slot], same, 8, 19)
+        send(tab_lse.at[j], home_lse.at[slot], same, 9, 20)
+        send(rows_of(j, other), home.at[slot], cross, 8, 19)
+        send(tab_lse.at[j], home_lse.at[slot], cross, 9, 20)
     column(s)
-    arrivals += [
-        send(rows_of(s, other), home.at[slot], sib), send(tab_lse.at[s], home_lse.at[slot], sib)
-    ]
-    for copy in via:
-        copy.wait_recv()
-    up_slot = core * RING + ring(s, -1)
-    dn_slot = core * RING + ring(s, 1)
-    arrivals += [
-        send(fwd.at[0], home.at[up_slot], s_up), send(fwd_lse.at[0], home_lse.at[up_slot], s_up),
-        send(fwd.at[1], home.at[dn_slot], s_dn_x), send(fwd_lse.at[1], home_lse.at[dn_slot], s_dn_x),
-    ]
+    send(rows_of(s, other), home.at[slot], sib, 8, 19)
+    send(tab_lse.at[s], home_lse.at[slot], sib, 9, 20)
     home[slot] = tab[s, pl.ds(pl.multiple_of(core * rows, rows), rows)]
     home_lse[slot] = tab_lse[s]
-    for copy in arrivals:
-        copy.wait_recv()
+    sources = 2 * RING
+    wait_bytes(home_lse.at[pl.ds(0, sources - 1)], recv_sem.at[20])
+    wait_bytes(home.at[pl.ds(0, sources - 1)], recv_sem.at[19])
 
     sub_r = lax.broadcasted_iota(jnp.int32, (rows, lane_n), 0)
     lane_r = lax.broadcasted_iota(jnp.int32, (rows, lane_n), 1)
     diag = lane_r == sub_r + core * rows
     new_value = new_kv[:, head_dim:].astype(f32)
     attention = []
-    sources = 2 * RING
     for h in range(heads):
         cols_h = [
             jnp.sum(jnp.where(diag, home_lse[n, h:h + 1, :], 0.0), axis=1, keepdims=True)
@@ -396,20 +349,26 @@
         attention.append((mixed / denominator).astype(bf16))
     att = jnp.concatenate(attention, axis=1)
 
-    tp_sends = []
     for k in (2, 1, 3):
         t = lax.rem(tp + k, RING)
         part[t] = jnp.dot(att, weight[t], preferred_element_type=f32).astype(bf16)
-        tp_sends.append(send(part.at[t], part_in.at[tp], tps[k - 1]))
+        send(part.at[t], part_in.at[tp], tps[k - 1], 10, 21)
     total = jnp.dot(att, weight[tp], preferred_element_type=f32) + residual[...].astype(f32)
-    for copy in tp_sends:
-        copy.wait_recv()
+    wait_bytes(part_in.at[pl.ds(0, RING - 1)], recv_sem.at[21])
     for k in range(1, RING):
         total = total + part_in[lax.rem(tp + k, RING)].astype(f32)
     out_ref[...] = total.astype(bf16)
 
-    for copy in started:
+    wait_bytes(q_all.at[pl.ds(0, 15)], send_sem.at[0])
+    order_to_sib.wait_send()
+    for copy in order_copies:
         copy.wait_send()
+    pick.wait_send()
+    wait_bytes(o_all.at[pl.ds(0, RING - 1)], send_sem.at[6])
+    wait_bytes(lse_all.at[pl.ds(0, RING - 1)], send_sem.at[7])
+    wait_bytes(home.at[pl.ds(0, sources - 1)], send_sem.at[8])
+    wait_bytes(home_lse.at[pl.ds(0, sources - 1)], send_sem.at[9])
+    wait_bytes(part_in.at[pl.ds(0, RING - 1)], send_sem.at[10])
 
 
 def local(residual, queries, new_kv, cache, out_weight, block_counts, last_fill, block_order):
@@ -422,7 +381,6 @@
     devices = requests // rows
     any_spec = pl.BlockSpec(memory_space=pl.ANY)
     f32, bf16 = jnp.float32, jnp.bfloat16
-    copies = 96
     return pl.pallas_call(
         kernel,
         out_shape=jax.ShapeDtypeStruct((rows, cols), bf16),
@@ -440,7 +398,10 @@
             pltpu.VMEM((devices, rows, q_cols), bf16),
             pltpu.VMEM((requests // lanes, lanes), f32),
             pltpu.VMEM((requests // lanes, lanes), f32),
-            pltpu.VMEM((num_blocks, requests), bf16),
+            pltpu.VMEM((2, num_blocks, requests), bf16),
+            pltpu.VMEM((1, num_blocks), jnp.int32),
+            pltpu.VMEM((num_blocks, q_cols), bf16),
+            pltpu.VMEM((num_blocks, q_cols), bf16),
             pltpu.VMEM((num_blocks, 8, head_dim), f32),
             pltpu.VMEM((num_blocks, 8, block_len), f32),
             pltpu.VMEM((num_blocks, 8, head_dim), f32),
@@ -448,16 +409,14 @@
             pltpu.VMEM((RING, 8, lanes), f32),
             pltpu.VMEM((RING, 2 * rows, q_cols), bf16),
             pltpu.VMEM((RING, 8, lanes), f32),
-            pltpu.VMEM((2, rows, q_cols), bf16),
-            pltpu.VMEM((2, 8, lanes), f32),
             pltpu.VMEM((2 * RING, rows, q_cols), bf16),
             pltpu.VMEM((2 * RING, 8, lanes), f32),
             pltpu.VMEM((RING, rows, cols), bf16),
             pltpu.VMEM((RING, rows, cols), bf16),
-            pltpu.SemaphoreType.DMA((copies,)),
-            pltpu.SemaphoreType.DMA((copies,)),
+            pltpu.SemaphoreType.DMA((11,)),
+            pltpu.SemaphoreType.DMA((22,)),
+            pltpu.SemaphoreType.DMA((GROUPS,)),
             pltpu.SemaphoreType.DMA((8,)),
-            pltpu.SemaphoreType.DMA((11,)),
         ],
         compiler_params=pltpu.CompilerParams(
             collective_id=0, has_side_effects=True, vmem_limit_bytes=60 * 1024 * 1024

time: 49.2 us -> 40.4 us (0.82); the launches traced: 48.5 us -> 40.3 us
  Pallas kernels: 47.1 us -> 38.9 us
    pallas_call x1, Pallas kernels: 47.1 us -> 38.9 us  [local(): pl.pallas_call(kernel, out_shape=jax.ShapeDtypeStruct((rows, cols), bf16)...]
where the time goes in v2:
time: 40.4 us; the launch traced here: 40.3 us
  Pallas kernels  38.9 us (96%)
  local copies, waits for them, and re-layouts  1.4 us (3%)
    pallas_call x1, Pallas kernels, local(): pl.pallas_call(kernel, out_shape=jax.ShapeDtypeStruct((rows, cols), bf16)...  38.9 us
    unnamed x1, local copies, waits for them, and re-layouts  1.4 us

profile of v2, /device:TPU:1, one launch (start us, length us, event | category | flops | bytes accessed | tf_op | source)
XLA Modules:
  0.0 40.3 jit_solution(2768935032915377251)
XLA Ops:
  0.0 38.9 %shard_map.82 = bf16[32,640]{1,0:T(8,128)(2,1)} custom-call(s32[1,64]{1,0:T(1,128)} %bitcast.5, s32[8,128]{1,0:T(8,128)} %bitcast.3, s32[8,128]{1,0:T(8,128)} %bitcast.4, bf16[32,640]{1,0:T(8,128)(2,1)} %residual_hbm.1, bf16[32,768]{1,0:T(8,128)(2,1)} %queries_hbm.1, bf16[32,512]{1,0:T(8,128)(2,1)} %new_kv_hbm.1, bf16[64,256,512]{2,1,0:T(8,128)(2,1)} %cache_hbm.1, ...), custom_call_target="tpu_custom_call" | custom-call | tf_op jit(solution)/shard_map/pallas_call | solution.py:384
  38.9 1.4 %copy.10 = bf16[32,640]{1,0:T(8,128)(2,1)} copy(bf16[32,640]{1,0:T(8,128)(2,1)} %shard_map.82) | data formatting | bytes 81920

commit v3 on v2

--- a/solution.py
+++ b/solution.py
@@ -14,8 +14,8 @@
 def kernel(
     order_hbm, counts_hbm, fill_hbm, residual_hbm, queries_hbm, new_kv_hbm, cache_hbm, weight_hbm,
     out_ref,
-    cache, weight, residual, new_kv, q_own, counts, fill, order_all, q_all, ends_ref, starts_ref,
-    onehot_ref, order_sib, pick_out, pick_in, q_blk, live, o_scr, o_all, lse_all, tab, tab_lse,
+    cache, weight, residual, new_kv, q_own, counts, fill, order_all, q_rel, ends_ref, starts_ref,
+    onehot_ref, early_ref, order_sib, pick_out, pick_in, q_blk, live, o_scr, o_all, lse_all, tab, tab_lse,
     home, home_lse, part, part_in, send_sem, recv_sem, cache_sem, local_sem,
 ):
     num_blocks, block_len, width = cache.shape
@@ -75,7 +75,7 @@
         pltpu.make_async_copy(fill_hbm, fill, local_sem.at[3]),
         pltpu.make_async_copy(new_kv_hbm, new_kv, local_sem.at[4]),
         pltpu.make_async_copy(residual_hbm, residual, local_sem.at[5]),
-        pltpu.make_async_copy(queries_hbm, q_all.at[me], local_sem.at[6]),
+        pltpu.make_async_copy(queries_hbm, q_rel.at[0], local_sem.at[6]),
     ]
     for copy in small:
         copy.start()
@@ -116,21 +116,20 @@
     half = rows // 2
     top, bottom = pl.ds(0, half), pl.ds(half, half)
 
-    def chunk(i, j):
-        return q_all.at[seq_of(ring(f, i), ring(s, j), core)]
-
-    def part_of(i, j, which):
-        return q_all.at[seq_of(ring(f, i), ring(s, j), core), which]
+    def place(i, j):
+        return (0, 2, 3, 1)[j % RING] * RING + i % RING
 
     def to_s(i, src=None):
-        c = chunk(i, 0)
-        src = c if src is None else src
+        src = q_rel.at[place(i, 0)] if src is None else src
         n = 3 + 2 * (i % RING)
-        return (send(src, c, s_up, 0, n), send(src, c, s_dn, 0, n + 1))
-
-    own_up = send(q_own, chunk(0, 0), f_up, 0, 0)
-    own_dn = send(q_own, chunk(0, 0), f_dn, 0, 1)
-    own_2 = send(q_own, chunk(0, 0), f_2, 0, 2)
+        return (
+            send(src, q_rel.at[place(i, -1)], s_up, 0, n),
+            send(src, q_rel.at[place(i, 1)], s_dn, 0, n + 1),
+        )
+
+    own_up = send(q_own, q_rel.at[place(-1, 0)], f_up, 0, 0)
+    own_dn = send(q_own, q_rel.at[place(1, 0)], f_dn, 0, 1)
+    own_2 = send(q_own, q_rel.at[place(2, 0)], f_2, 0, 2)
     s_copies = {0: to_s(0, q_own)}
 
     for copy in small:
@@ -167,23 +166,37 @@
             axis=1, keepdims=True,
         )
 
+    row_lane = lax.broadcasted_iota(jnp.int32, (num_blocks, RING * rows), 1)
+    row_ids = []
+    for j in (0, -1, 1, 2):
+        ids = row_lane
+        for i in range(RING):
+            base = seq_of(ring(f, i), ring(s, j), core) * rows - i * rows
+            here = (row_lane >= i * rows) & (row_lane < (i + 1) * rows)
+            ids = jnp.where(here, row_lane + base, ids)
+        row_ids.append(ids.astype(f32))
+
+    def select(which, order_col):
+        passed = jnp.zeros((num_blocks, lane_n), f32)
+        for k in range(pieces):
+            passed = passed + jnp.where(ends_ref[k:k + 1, :] <= order_col, 1.0, 0.0)
+        request = jnp.sum(passed, axis=1, keepdims=True)
+        for n in range(RING):
+            onehot_ref[which, :, n * RING * rows:(n + 1) * RING * rows] = (
+                jnp.where(row_ids[n] == request, 1.0, 0.0).astype(bf16)
+            )
+
     order_col = column_of(order_all[f].astype(f32))
     fill_raw = jnp.zeros((num_blocks, lane_n), f32)
     for k in range(pieces):
-        ends_k = ends_ref[k:k + 1, :]
-        starts_k = starts_ref[k:k + 1, :]
-        hit = (starts_k <= order_col) & (order_col < ends_k)
-        onehot_ref[0, :, k * lane_n:(k + 1) * lane_n] = jnp.where(hit, 1.0, 0.0).astype(bf16)
-        fill_raw = fill_raw + jnp.where(ends_k == order_col + 1.0, fill_f[k:k + 1, :], 0.0)
+        fill_raw = fill_raw + jnp.where(
+            ends_ref[k:k + 1, :] == order_col + 1.0, fill_f[k:k + 1, :], 0.0
+        )
     fill_sum = jnp.sum(fill_raw, axis=1, keepdims=True)
     live_n = jnp.where(fill_sum > 0.0, fill_sum, float(block_len))
+    select(0, order_col)
     order_to_sib.wait_recv()
-    order_col = column_of(order_sib[...].astype(f32))
-    for k in range(pieces):
-        hit = (starts_ref[k:k + 1, :] <= order_col) & (order_col < ends_ref[k:k + 1, :])
-        onehot_ref[1, :, k * lane_n:(k + 1) * lane_n] = jnp.where(hit, 1.0, 0.0).astype(bf16)
-    for n in range(RING * RING):
-        q_all[2 * n + other] = jnp.zeros((rows, heads * head_dim), bf16)
+    select(1, column_of(order_sib[...].astype(f32)))
     for h in range(8):
         live[:, h, :] = jnp.broadcast_to(live_n, (num_blocks, block_len))
     q_blk[...] = jnp.zeros(q_blk.shape, f32)
@@ -191,9 +204,9 @@
     def forward_s(i):
         up, dn = s_copies[i]
         up.wait_recv()
-        send(part_of(i, -1, top), part_of(i, -1, top), s_up, 0, 11)
+        send(q_rel.at[place(i, -1), top], q_rel.at[place(i, 2), top], s_up, 0, 11)
         dn.wait_recv()
-        send(part_of(i, 1, bottom), part_of(i, 1, bottom), s_dn, 0, 11)
+        send(q_rel.at[place(i, 1), bottom], q_rel.at[place(i, 2), bottom], s_dn, 0, 11)
 
     own_up.wait_recv()
     s_copies[-1] = to_s(-1)
@@ -205,16 +218,24 @@
     forward_s(-1)
     forward_s(1)
     forward_s(2)
-    wait_bytes(q_all.at[pl.ds(0, RING)], recv_sem.at[11])
-
-    q_rows = q_all[...].reshape(q_all.shape[0] * rows, heads * head_dim)
-    pick_out[...] = jnp.dot(onehot_ref[1], q_rows, preferred_element_type=f32).astype(bf16)
-    pick = send(pick_out, pick_in, sib, 5, 16)
-    picked = jnp.dot(onehot_ref[0], q_rows, preferred_element_type=f32)
-    pick.wait_recv()
-    picked = picked + pick_in[...].astype(f32)
-    for h in range(heads):
-        q_blk[:, h, :] = picked[:, h * head_dim:(h + 1) * head_dim]
+
+    early_n = (RING - 1) * RING
+    early = q_rel[0:early_n].reshape(early_n * rows, heads * head_dim)
+    for which in range(2):
+        early_ref[which] = jnp.dot(
+            onehot_ref[which, :, :early_n * rows], early, preferred_element_type=f32
+        )
+    wait_bytes(q_rel.at[pl.ds(0, RING)], recv_sem.at[11])
+    late = q_rel[early_n:].reshape(RING * rows, heads * head_dim)
+
+    def pick(which):
+        return early_ref[which] + jnp.dot(
+            onehot_ref[which, :, early_n * rows:], late, preferred_element_type=f32
+        )
+
+    pick_out[...] = pick(1).astype(bf16).reshape(pick_out.shape)
+    picks = [send(pick_out.at[g], pick_in.at[g], sib, 5, 16 + g) for g in range(GROUPS)]
+    early_ref[0] = pick(0)
 
     lse_all[f] = jnp.zeros((8, lane_n), f32)
     token = lax.broadcasted_iota(jnp.int32, (8, block_len), 1).astype(f32)
@@ -222,6 +243,11 @@
 
     for g in range(GROUPS):
         cache_copies[g].wait()
+        picks[g].wait_recv()
+        first = g * per_group
+        picked = early_ref[0, first:first + per_group, :] + pick_in[g].astype(f32)
+        for h in range(heads):
+            q_blk[first:first + per_group, h, :] = picked[:, h * head_dim:(h + 1) * head_dim]
         blocks = range(g * per_group, (g + 1) * per_group)
         lse_rows = lse_all[f]
         scores = []
@@ -248,10 +274,10 @@
             )
         ref = o_all.at[f, g]
         for peer in (f_2, f_up, f_dn):
-            send(ref, ref, peer, 6, 17)
+            send(ref, ref, peer, 6, 20)
     ref = lse_all.at[f]
     for peer in (f_2, f_up, f_dn):
-        send(ref, ref, peer, 7, 18)
+        send(ref, ref, peer, 7, 21)
 
     q_f = q_own[...].astype(f32)
     new_key = new_kv[:, :head_dim].astype(f32)
@@ -262,8 +288,8 @@
     wait_bytes(weight, local_sem.at[7])
     for copy in order_copies:
         copy.wait_recv()
-    wait_bytes(lse_all.at[pl.ds(0, RING - 1)], recv_sem.at[18])
-    wait_bytes(o_all.at[pl.ds(0, RING - 1)], recv_sem.at[17])
+    wait_bytes(lse_all.at[pl.ds(0, RING - 1)], recv_sem.at[21])
+    wait_bytes(o_all.at[pl.ds(0, RING - 1)], recv_sem.at[20])
 
     def pair(a, b):
         lanes = lax.broadcasted_iota(jnp.int32, a.shape, 1)
@@ -314,18 +340,18 @@
     for k, same, cross in ((2, s_2, s_2_x), (1, s_up, s_up_x), (-1, s_dn, s_dn_x)):
         j = ring(s, k)
         column(j)
-        send(rows_of(j, core), home.at[slot], same, 8, 19)
-        send(tab_lse.at[j], home_lse.at[slot], same, 9, 20)
-        send(rows_of(j, other), home.at[slot], cross, 8, 19)
-        send(tab_lse.at[j], home_lse.at[slot], cross, 9, 20)
+        send(rows_of(j, core), home.at[slot], same, 8, 22)
+        send(tab_lse.at[j], home_lse.at[slot], same, 9, 23)
+        send(rows_of(j, other), home.at[slot], cross, 8, 22)
+        send(tab_lse.at[j], home_lse.at[slot], cross, 9, 23)
     column(s)
-    send(rows_of(s, other), home.at[slot], sib, 8, 19)
-    send(tab_lse.at[s], home_lse.at[slot], sib, 9, 20)
+    send(rows_of(s, other), home.at[slot], sib, 8, 22)
+    send(tab_lse.at[s], home_lse.at[slot], sib, 9, 23)
     home[slot] = tab[s, pl.ds(pl.multiple_of(core * rows, rows), rows)]
     home_lse[slot] = tab_lse[s]
     sources = 2 * RING
-    wait_bytes(home_lse.at[pl.ds(0, sources - 1)], recv_sem.at[20])
-    wait_bytes(home.at[pl.ds(0, sources - 1)], recv_sem.at[19])
+    wait_bytes(home_lse.at[pl.ds(0, sources - 1)], recv_sem.at[23])
+    wait_bytes(home.at[pl.ds(0, sources - 1)], recv_sem.at[22])
 
     sub_r = lax.broadcasted_iota(jnp.int32, (rows, lane_n), 0)
     lane_r = lax.broadcasted_iota(jnp.int32, (rows, lane_n), 1)
@@ -352,18 +378,18 @@
     for k in (2, 1, 3):
         t = lax.rem(tp + k, RING)
         part[t] = jnp.dot(att, weight[t], preferred_element_type=f32).astype(bf16)
-        send(part.at[t], part_in.at[tp], tps[k - 1], 10, 21)
+        send(part.at[t], part_in.at[tp], tps[k - 1], 10, 24)
     total = jnp.dot(att, weight[tp], preferred_element_type=f32) + residual[...].astype(f32)
-    wait_bytes(part_in.at[pl.ds(0, RING - 1)], recv_sem.at[21])
+    wait_bytes(part_in.at[pl.ds(0, RING - 1)], recv_sem.at[24])
     for k in range(1, RING):
         total = total + part_in[lax.rem(tp + k, RING)].astype(f32)
     out_ref[...] = total.astype(bf16)
 
-    wait_bytes(q_all.at[pl.ds(0, 15)], send_sem.at[0])
+    wait_bytes(q_rel.at[pl.ds(0, 15)], send_sem.at[0])
     order_to_sib.wait_send()
     for copy in order_copies:
         copy.wait_send()
-    pick.wait_send()
+    wait_bytes(pick_out, send_sem.at[5])
     wait_bytes(o_all.at[pl.ds(0, RING - 1)], send_sem.at[6])
     wait_bytes(lse_all.at[pl.ds(0, RING - 1)], send_sem.at[7])
     wait_bytes(home.at[pl.ds(0, sources - 1)], send_sem.at[8])
@@ -378,7 +404,6 @@
     q_cols = queries.shape[1]
     requests = block_counts.shape[0]
     lanes = 128
-    devices = requests // rows
     any_spec = pl.BlockSpec(memory_space=pl.ANY)
     f32, bf16 = jnp.float32, jnp.bfloat16
     return pl.pallas_call(
@@ -395,13 +420,14 @@
             pltpu.VMEM((requests // lanes, lanes), jnp.int32),
             pltpu.VMEM((requests // lanes, lanes), jnp.int32),
             pltpu.VMEM((RING, 1, num_blocks), jnp.int32),
-            pltpu.VMEM((devices, rows, q_cols), bf16),
+            pltpu.VMEM((RING * RING, rows, q_cols), bf16),
             pltpu.VMEM((requests // lanes, lanes), f32),
             pltpu.VMEM((requests // lanes, lanes), f32),
-            pltpu.VMEM((2, num_blocks, requests), bf16),
+            pltpu.VMEM((2, num_blocks, requests // 2), bf16),
+            pltpu.VMEM((2, num_blocks, q_cols), f32),
             pltpu.VMEM((1, num_blocks), jnp.int32),
-            pltpu.VMEM((num_blocks, q_cols), bf16),
-            pltpu.VMEM((num_blocks, q_cols), bf16),
+            pltpu.VMEM((GROUPS, num_blocks // GROUPS, q_cols), bf16),
+            pltpu.VMEM((GROUPS, num_blocks // GROUPS, q_cols), bf16),
             pltpu.VMEM((num_blocks, 8, head_dim), f32),
             pltpu.VMEM((num_blocks, 8, block_len), f32),
             pltpu.VMEM((num_blocks, 8, head_dim), f32),
@@ -414,7 +440,7 @@
             pltpu.VMEM((RING, rows, cols), bf16),
             pltpu.VMEM((RING, rows, cols), bf16),
             pltpu.SemaphoreType.DMA((11,)),
-            pltpu.SemaphoreType.DMA((22,)),
+            pltpu.SemaphoreType.DMA((25,)),
             pltpu.SemaphoreType.DMA((GROUPS,)),
             pltpu.SemaphoreType.DMA((8,)),
         ],

time: 40.4 us -> 40 us (0.990)
  Pallas kernels: 38.9 us -> 38.4 us
    pallas_call x1, Pallas kernels: 38.9 us -> 38.4 us  [local(): pl.pallas_call(kernel, out_shape=jax.ShapeDtypeStruct((rows, cols), bf16)...]
where the time goes in v3:
time: 40 us; the launch traced here: 39.8 us
  Pallas kernels  38.4 us (96%)
  local copies, waits for them, and re-layouts  1.4 us (4%)
    pallas_call x1, Pallas kernels, local(): pl.pallas_call(kernel, out_shape=jax.ShapeDtypeStruct((rows, cols), bf16)...  38.4 us
    unnamed x1, local copies, waits for them, and re-layouts  1.4 us

profile of v3, /device:TPU:1, one launch (start us, length us, event | category | flops | bytes accessed | tf_op | source)
XLA Modules:
  0.0 39.8 jit_solution(2440589962584452634)
XLA Ops:
  0.0 38.4 %shard_map.82 = bf16[32,640]{1,0:T(8,128)(2,1)} custom-call(s32[1,64]{1,0:T(1,128)} %bitcast.5, s32[8,128]{1,0:T(8,128)} %bitcast.3, s32[8,128]{1,0:T(8,128)} %bitcast.4, bf16[32,640]{1,0:T(8,128)(2,1)} %residual_hbm.1, bf16[32,768]{1,0:T(8,128)(2,1)} %queries_hbm.1, bf16[32,512]{1,0:T(8,128)(2,1)} %new_kv_hbm.1, bf16[64,256,512]{2,1,0:T(8,128)(2,1)} %cache_hbm.1, ...), custom_call_target="tpu_custom_call" | custom-call | tf_op jit(solution)/shard_map/pallas_call | solution.py:409
  38.4 1.4 %copy.10 = bf16[32,640]{1,0:T(8,128)(2,1)} copy(bf16[32,640]{1,0:T(8,128)(2,1)} %shard_map.82) | data formatting | bytes 81920

commit v4 on v3

--- a/solution.py
+++ b/solution.py
@@ -67,6 +67,14 @@
     for peer in peers:
         pl.semaphore_signal(barrier, inc=1, device_id=peer, device_id_type=MESH)
 
+    half = rows // 2
+    early_n = (RING - 1) * RING
+    axes = ((f_up, f_dn, f_2, s_up, s_dn), (s_up, s_dn, s_2, f_up, f_dn))
+
+    def slot_of(h, i, j):
+        n = (0, 2, 3, 1)[j % RING] * RING + i % RING
+        return h * early_n + n if n < early_n else early_n + n + h * RING
+
     own_q = pltpu.make_async_copy(queries_hbm, q_own, local_sem.at[0])
     own_q.start()
     small = [
@@ -75,7 +83,11 @@
         pltpu.make_async_copy(fill_hbm, fill, local_sem.at[3]),
         pltpu.make_async_copy(new_kv_hbm, new_kv, local_sem.at[4]),
         pltpu.make_async_copy(residual_hbm, residual, local_sem.at[5]),
-        pltpu.make_async_copy(queries_hbm, q_rel.at[0], local_sem.at[6]),
+    ] + [
+        pltpu.make_async_copy(
+            queries_hbm.at[pl.ds(h * half, half)], q_rel.at[slot_of(h, 0, 0)], local_sem.at[6 + h]
+        )
+        for h in range(2)
     ]
     for copy in small:
         copy.start()
@@ -92,7 +104,7 @@
         copy.start()
     weight_copies = [
         pltpu.make_async_copy(
-            weight_hbm.at[:, pl.ds(t * cols, cols)], weight.at[t], local_sem.at[7]
+            weight_hbm.at[:, pl.ds(t * cols, cols)], weight.at[t], local_sem.at[8]
         )
         for t in range(RING)
     ]
@@ -113,31 +125,31 @@
     own_q.wait()
     pl.semaphore_wait(barrier, len(peers))
 
-    half = rows // 2
-    top, bottom = pl.ds(0, half), pl.ds(half, half)
-
-    def place(i, j):
-        return (0, 2, 3, 1)[j % RING] * RING + i % RING
-
-    def to_s(i, src=None):
-        src = q_rel.at[place(i, 0)] if src is None else src
-        n = 3 + 2 * (i % RING)
+    def to_b(h, i, src=None):
+        b_up, b_dn = axes[h][3:]
+        src = q_rel.at[slot_of(h, i, 0)] if src is None else src
+        n = 11 * h + 3 + 2 * (i % RING)
         return (
-            send(src, q_rel.at[place(i, -1)], s_up, 0, n),
-            send(src, q_rel.at[place(i, 1)], s_dn, 0, n + 1),
-        )
-
-    own_up = send(q_own, q_rel.at[place(-1, 0)], f_up, 0, 0)
-    own_dn = send(q_own, q_rel.at[place(1, 0)], f_dn, 0, 1)
-    own_2 = send(q_own, q_rel.at[place(2, 0)], f_2, 0, 2)
-    s_copies = {0: to_s(0, q_own)}
+            send(src, q_rel.at[slot_of(h, i, -1)], b_up, 0, n),
+            send(src, q_rel.at[slot_of(h, i, 1)], b_dn, 0, n + 1),
+        )
+
+    own = [q_own.at[pl.ds(h * half, half)] for h in range(2)]
+    firsts = [
+        [
+            send(own[h], q_rel.at[slot_of(h, i, 0)], peer, 0, 11 * h + k)
+            for k, (i, peer) in enumerate(zip((-1, 1, 2), axes[h]))
+        ]
+        for h in range(2)
+    ]
+    b_copies = {(h, 0): to_b(h, 0, own[h]) for h in range(2)}
 
     for copy in small:
         copy.wait()
     order_own = order_all.at[f]
-    order_to_sib = send(order_own, order_sib, sib, 1, 12)
+    order_to_sib = send(order_own, order_sib, sib, 1, 23)
     order_copies = [
-        send(order_own, order_own, peer, 2 + k, 13 + k) for k, peer in enumerate((f_up, f_dn, f_2))
+        send(order_own, order_own, peer, 2 + k, 24 + k) for k, peer in enumerate((f_up, f_dn, f_2))
     ]
 
     counts_f = counts[...].astype(f32)
@@ -166,13 +178,18 @@
             axis=1, keepdims=True,
         )
 
-    row_lane = lax.broadcasted_iota(jnp.int32, (num_blocks, RING * rows), 1)
+    places_of = {
+        slot_of(h, i, j): (h, i, j) for h in range(2) for i in range(RING) for j in range(RING)
+    }
+    row_lane = lax.broadcasted_iota(jnp.int32, (1, RING * rows), 1)
     row_ids = []
-    for j in (0, -1, 1, 2):
+    for n in range(RING):
         ids = row_lane
-        for i in range(RING):
-            base = seq_of(ring(f, i), ring(s, j), core) * rows - i * rows
-            here = (row_lane >= i * rows) & (row_lane < (i + 1) * rows)
+        for k in range(2 * RING):
+            h, i, j = places_of[n * 2 * RING + k]
+            fi, si = (i, j) if h == 0 else (j, i)
+            base = seq_of(ring(f, fi), ring(s, si), core) * rows + h * half - k * half
+            here = (row_lane >= k * half) & (row_lane < (k + 1) * half)
             ids = jnp.where(here, row_lane + base, ids)
         row_ids.append(ids.astype(f32))
 
@@ -201,32 +218,32 @@
         live[:, h, :] = jnp.broadcast_to(live_n, (num_blocks, block_len))
     q_blk[...] = jnp.zeros(q_blk.shape, f32)
 
-    def forward_s(i):
-        up, dn = s_copies[i]
+    left, right = pl.ds(0, heads * head_dim // 2), pl.ds(heads * head_dim // 2, heads * head_dim // 2)
+
+    def forward_b(h, i):
+        b_up, b_dn = axes[h][3:]
+        up, dn = b_copies[h, i]
+        to = slot_of(h, i, 2)
         up.wait_recv()
-        send(q_rel.at[place(i, -1), top], q_rel.at[place(i, 2), top], s_up, 0, 11)
+        send(q_rel.at[slot_of(h, i, -1), :, left], q_rel.at[to, :, left], b_up, 0, 22)
         dn.wait_recv()
-        send(q_rel.at[place(i, 1), bottom], q_rel.at[place(i, 2), bottom], s_dn, 0, 11)
-
-    own_up.wait_recv()
-    s_copies[-1] = to_s(-1)
-    own_dn.wait_recv()
-    s_copies[1] = to_s(1)
-    forward_s(0)
-    own_2.wait_recv()
-    s_copies[2] = to_s(2)
-    forward_s(-1)
-    forward_s(1)
-    forward_s(2)
-
-    early_n = (RING - 1) * RING
-    early = q_rel[0:early_n].reshape(early_n * rows, heads * head_dim)
+        send(q_rel.at[slot_of(h, i, 1), :, right], q_rel.at[to, :, right], b_dn, 0, 22)
+
+    for k, i in enumerate((-1, 1, 2)):
+        for h in range(2):
+            firsts[h][k].wait_recv()
+            b_copies[h, i] = to_b(h, i)
+    for i in (0, -1, 1, 2):
+        for h in range(2):
+            forward_b(h, i)
+
+    early = q_rel[0:2 * early_n].reshape(early_n * rows, heads * head_dim)
     for which in range(2):
         early_ref[which] = jnp.dot(
             onehot_ref[which, :, :early_n * rows], early, preferred_element_type=f32
         )
-    wait_bytes(q_rel.at[pl.ds(0, RING)], recv_sem.at[11])
-    late = q_rel[early_n:].reshape(RING * rows, heads * head_dim)
+    wait_bytes(q_rel.at[pl.ds(0, 2 * RING)], recv_sem.at[22])
+    late = q_rel[2 * early_n:].reshape(RING * rows, heads * head_dim)
 
     def pick(which):
         return early_ref[which] + jnp.dot(
@@ -234,7 +251,7 @@
         )
 
     pick_out[...] = pick(1).astype(bf16).reshape(pick_out.shape)
-    picks = [send(pick_out.at[g], pick_in.at[g], sib, 5, 16 + g) for g in range(GROUPS)]
+    picks = [send(pick_out.at[g], pick_in.at[g], sib, 5, 27 + g) for g in range(GROUPS)]
     early_ref[0] = pick(0)
 
     lse_all[f] = jnp.zeros((8, lane_n), f32)
@@ -274,10 +291,10 @@
             )
         ref = o_all.at[f, g]
         for peer in (f_2, f_up, f_dn):
-            send(ref, ref, peer, 6, 20)
+            send(ref, ref, peer, 6, 31)
     ref = lse_all.at[f]
     for peer in (f_2, f_up, f_dn):
-        send(ref, ref, peer, 7, 21)
+        send(ref, ref, peer, 7, 32)
 
     q_f = q_own[...].astype(f32)
     new_key = new_kv[:, :head_dim].astype(f32)
@@ -285,11 +302,11 @@
         jnp.sum(q_f[:, h * head_dim:(h + 1) * head_dim] * new_key, axis=1, keepdims=True) * inv_root
         for h in range(heads)
     ]
-    wait_bytes(weight, local_sem.at[7])
+    wait_bytes(weight, local_sem.at[8])
     for copy in order_copies:
         copy.wait_recv()
-    wait_bytes(lse_all.at[pl.ds(0, RING - 1)], recv_sem.at[21])
-    wait_bytes(o_all.at[pl.ds(0, RING - 1)], recv_sem.at[20])
+    wait_bytes(lse_all.at[pl.ds(0, RING - 1)], recv_sem.at[32])
+    wait_bytes(o_all.at[pl.ds(0, RING - 1)], recv_sem.at[31])
 
     def pair(a, b):
         lanes = lax.broadcasted_iota(jnp.int32, a.shape, 1)
@@ -340,18 +357,18 @@
     for k, same, cross in ((2, s_2, s_2_x), (1, s_up, s_up_x), (-1, s_dn, s_dn_x)):
         j = ring(s, k)
         column(j)
-        send(rows_of(j, core), home.at[slot], same, 8, 22)
-        send(tab_lse.at[j], home_lse.at[slot], same, 9, 23)
-        send(rows_of(j, other), home.at[slot], cross, 8, 22)
-        send(tab_lse.at[j], home_lse.at[slot], cross, 9, 23)
+        send(rows_of(j, core), home.at[slot], same, 8, 33)
+        send(tab_lse.at[j], home_lse.at[slot], same, 9, 34)
+        send(rows_of(j, other), home.at[slot], cross, 8, 33)
+        send(tab_lse.at[j], home_lse.at[slot], cross, 9, 34)
     column(s)
-    send(rows_of(s, other), home.at[slot], sib, 8, 22)
-    send(tab_lse.at[s], home_lse.at[slot], sib, 9, 23)
+    send(rows_of(s, other), home.at[slot], sib, 8, 33)
+    send(tab_lse.at[s], home_lse.at[slot], sib, 9, 34)
     home[slot] = tab[s, pl.ds(pl.multiple_of(core * rows, rows), rows)]
     home_lse[slot] = tab_lse[s]
     sources = 2 * RING
-    wait_bytes(home_lse.at[pl.ds(0, sources - 1)], recv_sem.at[23])
-    wait_bytes(home.at[pl.ds(0, sources - 1)], recv_sem.at[22])
+    wait_bytes(home_lse.at[pl.ds(0, sources - 1)], recv_sem.at[34])
+    wait_bytes(home.at[pl.ds(0, sources - 1)], recv_sem.at[33])
 
     sub_r = lax.broadcasted_iota(jnp.int32, (rows, lane_n), 0)
     lane_r = lax.broadcasted_iota(jnp.int32, (rows, lane_n), 1)
@@ -378,14 +395,14 @@
     for k in (2, 1, 3):
         t = lax.rem(tp + k, RING)
         part[t] = jnp.dot(att, weight[t], preferred_element_type=f32).astype(bf16)
-        send(part.at[t], part_in.at[tp], tps[k - 1], 10, 24)
+        send(part.at[t], part_in.at[tp], tps[k - 1], 10, 35)
     total = jnp.dot(att, weight[tp], preferred_element_type=f32) + residual[...].astype(f32)
-    wait_bytes(part_in.at[pl.ds(0, RING - 1)], recv_sem.at[24])
+    wait_bytes(part_in.at[pl.ds(0, RING - 1)], recv_sem.at[35])
     for k in range(1, RING):
         total = total + part_in[lax.rem(tp + k, RING)].astype(f32)
     out_ref[...] = total.astype(bf16)
 
-    wait_bytes(q_rel.at[pl.ds(0, 15)], send_sem.at[0])
+    wait_bytes(q_rel.at[pl.ds(0, 30)], send_sem.at[0])
     order_to_sib.wait_send()
     for copy in order_copies:
         copy.wait_send()
@@ -420,7 +437,7 @@
             pltpu.VMEM((requests // lanes, lanes), jnp.int32),
             pltpu.VMEM((requests // lanes, lanes), jnp.int32),
             pltpu.VMEM((RING, 1, num_blocks), jnp.int32),
-            pltpu.VMEM((RING * RING, rows, q_cols), bf16),
+            pltpu.VMEM((2 * RING * RING, rows // 2, q_cols), bf16),
             pltpu.VMEM((requests // lanes, lanes), f32),
             pltpu.VMEM((requests // lanes, lanes), f32),
             pltpu.VMEM((2, num_blocks, requests // 2), bf16),
@@ -440,9 +457,9 @@
             pltpu.VMEM((RING, rows, cols), bf16),
             pltpu.VMEM((RING, rows, cols), bf16),
             pltpu.SemaphoreType.DMA((11,)),
-            pltpu.SemaphoreType.DMA((25,)),
+            pltpu.SemaphoreType.DMA((36,)),
             pltpu.SemaphoreType.DMA((GROUPS,)),
-            pltpu.SemaphoreType.DMA((8,)),
+            pltpu.SemaphoreType.DMA((9,)),
         ],
         compiler_params=pltpu.CompilerParams(
             collective_id=0, has_side_effects=True, vmem_limit_bytes=60 * 1024 * 1024

time: 40 us -> 39.5 us (0.988)
  Pallas kernels: 38.4 us -> 37.9 us
    pallas_call x1, Pallas kernels: 38.4 us -> 37.9 us  [local(): pl.pallas_call(kernel, out_shape=jax.ShapeDtypeStruct((rows, cols), bf16)...]
where the time goes in v4:
time: 39.5 us; the launch traced here: 39.3 us
  Pallas kernels  37.9 us (96%)
  local copies, waits for them, and re-layouts  1.4 us (4%)
    pallas_call x1, Pallas kernels, local(): pl.pallas_call(kernel, out_shape=jax.ShapeDtypeStruct((rows, cols), bf16)...  37.9 us
    unnamed x1, local copies, waits for them, and re-layouts  1.4 us

profile of v4, /device:TPU:1, one launch (start us, length us, event | category | flops | bytes accessed | tf_op | source)
XLA Modules:
  0.0 39.3 jit_solution(3168429461416106823)
XLA Ops:
  0.0 37.9 %shard_map.82 = bf16[32,640]{1,0:T(8,128)(2,1)} custom-call(s32[1,64]{1,0:T(1,128)} %bitcast.5, s32[8,128]{1,0:T(8,128)} %bitcast.3, s32[8,128]{1,0:T(8,128)} %bitcast.4, bf16[32,640]{1,0:T(8,128)(2,1)} %residual_hbm.1, bf16[32,768]{1,0:T(8,128)(2,1)} %queries_hbm.1, bf16[32,512]{1,0:T(8,128)(2,1)} %new_kv_hbm.1, bf16[64,256,512]{2,1,0:T(8,128)(2,1)} %cache_hbm.1, ...), custom_call_target="tpu_custom_call" | custom-call | tf_op jit(solution)/shard_map/pallas_call | solution.py:426
  37.9 1.4 %copy.10 = bf16[32,640]{1,0:T(8,128)(2,1)} copy(bf16[32,640]{1,0:T(8,128)(2,1)} %shard_map.82) | data formatting | bytes 81920

commit v5 on v4

--- a/solution.py
+++ b/solution.py
@@ -138,7 +138,7 @@
     firsts = [
         [
             send(own[h], q_rel.at[slot_of(h, i, 0)], peer, 0, 11 * h + k)
-            for k, (i, peer) in enumerate(zip((-1, 1, 2), axes[h]))
+            for k, (i, peer) in enumerate(zip((2, -1, 1), (axes[h][2], axes[h][0], axes[h][1])))
         ]
         for h in range(2)
     ]
@@ -229,7 +229,7 @@
         dn.wait_recv()
         send(q_rel.at[slot_of(h, i, 1), :, right], q_rel.at[to, :, right], b_dn, 0, 22)
 
-    for k, i in enumerate((-1, 1, 2)):
+    for k, i in ((1, -1), (2, 1), (0, 2)):
         for h in range(2):
             firsts[h][k].wait_recv()
             b_copies[h, i] = to_b(h, i)

time: 39.5 us -> 39.8 us (level)
  no operation moved by 1% of the time
where the time goes in v5:
time: 39.8 us; the launch traced here: 39.6 us
  Pallas kernels  38.2 us (96%)
  local copies, waits for them, and re-layouts  1.4 us (4%)
    pallas_call x1, Pallas kernels, local(): pl.pallas_call(kernel, out_shape=jax.ShapeDtypeStruct((rows, cols), bf16)...  38.2 us
    unnamed x1, local copies, waits for them, and re-layouts  1.4 us

profile of v5, /device:TPU:1, one launch (start us, length us, event | category | flops | bytes accessed | tf_op | source)
XLA Modules:
  0.0 39.6 jit_solution(1776905106401176743)
XLA Ops:
  0.0 38.2 %shard_map.82 = bf16[32,640]{1,0:T(8,128)(2,1)} custom-call(s32[1,64]{1,0:T(1,128)} %bitcast.5, s32[8,128]{1,0:T(8,128)} %bitcast.3, s32[8,128]{1,0:T(8,128)} %bitcast.4, bf16[32,640]{1,0:T(8,128)(2,1)} %residual_hbm.1, bf16[32,768]{1,0:T(8,128)(2,1)} %queries_hbm.1, bf16[32,512]{1,0:T(8,128)(2,1)} %new_kv_hbm.1, bf16[64,256,512]{2,1,0:T(8,128)(2,1)} %cache_hbm.1, ...), custom_call_target="tpu_custom_call" | custom-call | tf_op jit(solution)/shard_map/pallas_call | solution.py:426
  38.2 1.4 %copy.10 = bf16[32,640]{1,0:T(8,128)(2,1)} copy(bf16[32,640]{1,0:T(8,128)(2,1)} %shard_map.82) | data formatting | bytes 81920
